TPU v7x, 128 devices: a whole 4x4x4 slice. The times are simulated.
128 devices in a mesh: row: 16 (over z, x), col: 8 (over y, core).
Axes of the slice: x: 4, y: 4, z: 4, core: 2. Of those that a mesh axis runs over, the one named last changes fastest.
Arguments:
- inputs: bfloat16 [1536, 28672], P('col', 'row'), may hold values from -100 to 100
- out_grads: bfloat16 [1536, 8192], P('row', 'col'), may hold values from -30 to 30
- user_ids: int32 [4], replicated, may hold values from 0 to 1, as said below
Outputs:
- orthogonalized: bfloat16 [28672, 8192], P('row', 'col')
Inputs may be any that keep to these rules, and one draw needn't show every extreme that they name: `user_ids`: entry m is the user of microbatch m (rows m * 384 to (m + 1) * 384 - 1); each of the users 0 and 1 has exactly 2 microbatches.
All inputs are finite; a program needn't handle non-finite values.
Results may differ from a plain program's by a relative error of at most 0.0067.
Values may be sent and summed in bfloat16 or wider, within the bound.
A program may use at most 192 MiB of HBM per device.

v0:
```python
import math

import jax
import jax.numpy as jnp
from jax import lax
from jax.sharding import Mesh
from jax.sharding import PartitionSpec as P

FF = 28672
D = 8192
BLOCK = 1024
MICRO = 4
MB_ROWS = 384
NS_STEPS = 2
ROW = ("row_0", "row_1")
COL = ("col_0", "col_1")
ROW_COL = ("row_0", "row_1", "col_0", "col_1")


target_coef = 0.15


def one_axis_at_a_time(value, axes):
    for axis in axes:
        value = lax.psum(value, axis)
    return value


def shifted(value, axis, by):
    count = lax.axis_size(axis)
    pairs = [(i, i + by) for i in range(count) if 0 <= i + by < count]
    return lax.ppermute(value, axis, pairs)


def row_owner(user_ids, count):
    token_index = jnp.arange(count, dtype=jnp.int32)
    batch_index = token_index // MB_ROWS
    matches = batch_index[:, None] == jnp.arange(MICRO, dtype=jnp.int32)[None, :]
    return jnp.sum(jnp.where(matches, user_ids[None, :], 0), axis=1)


def contract(input_rows, grad_rows):
    return lax.dot_general(
        input_rows, grad_rows, (((0,), (0,)), ((), ())), preferred_element_type=jnp.float32
    )


def add_piece(carried, input_rows, grad_rows, user_ids):
    owners = row_owner(user_ids, input_rows.shape[0])
    leading = owners[0]
    uniform = jnp.all(owners == leading)

    def single(running_sum):
        product = contract(input_rows, grad_rows)
        current = lax.dynamic_index_in_dim(running_sum, leading, 0, keepdims=False)
        return lax.dynamic_update_index_in_dim(running_sum, current + product, leading, 0)

    def mingled(running_sum):
        in_second = (owners == 1)[:, None]
        nothing = jnp.zeros_like(grad_rows)
        for_zero = contract(input_rows, jnp.where(in_second, nothing, grad_rows))
        for_one = contract(input_rows, jnp.where(in_second, grad_rows, nothing))
        return jnp.stack([for_zero, for_one])

    return lax.cond(uniform, single, mingled, carried)


def newton(blocks):
    iterate = blocks
    for iteration in range(NS_STEPS):
        gram_matrix = jnp.einsum(
            "sibj,skbj->sbik", iterate, iterate, preferred_element_type=jnp.float32
        ).astype(jnp.bfloat16)
        product = jnp.einsum(
            "sbik,skbj->sibj", gram_matrix, iterate, preferred_element_type=jnp.float32
        )
        updated = 1.5 * iterate.astype(jnp.float32) - 0.5 * product
        if iteration == NS_STEPS - 1:
            updated = updated * math.sqrt(BLOCK)
        iterate = updated.astype(jnp.bfloat16)
    return iterate


def per_device(inputs, out_grads, user_ids):
    tile_rows = inputs.shape[1]
    tile_cols = out_grads.shape[1]
    running = jnp.zeros((2, tile_rows, tile_cols), jnp.float32)
    grads_whole = lax.all_gather(out_grads, ROW, axis=0, tiled=True)
    both_users = add_piece(
        running, lax.all_gather(inputs, COL, axis=0, tiled=True), grads_whole, user_ids
    )
    user_grads = both_users.astype(jnp.bfloat16)
    grad_zero = user_grads[0]
    grad_one = user_grads[1]
    squares = (
        jnp.sum(jnp.square(grad_zero.astype(jnp.float32))),
        jnp.sum(jnp.square(grad_one.astype(jnp.float32))),
    )
    totals = (one_axis_at_a_time(squares[0], ROW_COL), one_axis_at_a_time(squares[1], ROW_COL))
    target = target_coef * math.sqrt(FF * D / BLOCK)
    factor_zero = target / jnp.sqrt(totals[0] + 1e-06)
    factor_one = target / jnp.sqrt(totals[1] + 1e-06)
    blended = factor_zero * grad_zero.astype(jnp.float32) + factor_one * grad_one.astype(
        jnp.float32
    )
    update = blended.astype(jnp.bfloat16)
    next_head = shifted(update[:BLOCK], ROW, -1)
    extended = jnp.concatenate([update, next_head], axis=0)
    position = lax.axis_index(ROW)
    tile_start = position * tile_rows
    first_block = (tile_start + BLOCK - 1) // BLOCK
    slot_count = (tile_rows + BLOCK - 1) // BLOCK
    column_blocks = tile_cols // BLOCK
    slot_rows = []
    slot_valid = []
    slot_blocks = []
    for slot in range(slot_count):
        block_start = (first_block + slot) * BLOCK - tile_start
        slot_valid.append(block_start < tile_rows)
        local_row = jnp.minimum(block_start, tile_rows)
        slot_rows.append(local_row)
        block_rows = lax.dynamic_slice_in_dim(extended, local_row, BLOCK, 0)
        slot_blocks.append(block_rows.reshape(BLOCK, column_blocks, BLOCK))
    finished = newton(jnp.stack(slot_blocks))
    placed = jnp.zeros_like(extended)
    for slot in range(slot_count):
        current = lax.dynamic_slice_in_dim(placed, slot_rows[slot], BLOCK, 0)
        fresh = finished[slot].reshape(BLOCK, tile_cols)
        placed = lax.dynamic_update_slice_in_dim(
            placed, jnp.where(slot_valid[slot], fresh, current), slot_rows[slot], 0
        )
    tail_rows = shifted(placed[tile_rows:], ROW, 1)
    head_length = first_block * BLOCK - tile_start
    from_previous = jnp.arange(BLOCK, dtype=jnp.int32)[:, None] < head_length
    head_rows = jnp.where(from_previous, tail_rows, placed[:BLOCK])
    return jnp.concatenate([head_rows, placed[BLOCK:tile_rows]], axis=0)


def solution(mesh):
    torus = Mesh(mesh.devices.reshape(4, 4, 4, 2), ("row_0", "row_1", "col_0", "col_1"))
    return jax.shard_map(
        per_device,
        mesh=torus,
        in_specs=(P(COL, ROW), P(ROW, COL), P()),
        out_specs=P(ROW, COL),
        check_vma=False,
    )
```

profile of v0, /device:TPU:1, one launch (start us, length us, event | category | flops | bytes accessed | tf_op | source)
XLA Modules:
  0.0 346.4 jit_solution(17695000950454978052)
XLA Ops:
  11.3 48.7 %all-gather.3.cloned.1.call-done = bf16[1536,1024]{1,0:T(8,128)(2,1)} async-done(((bf16[96,1024]{1,0:T(8,128)(2,1)}), bf16[1536,1024]{1,0:T(8,128)(2,1)}) %all-gather.3.cloned.1.call-update) | async-done | bytes 3145744 | tf_op jit(solution)/shard_map/all_gather | solution.py:88
  60.0 39.0 %all-gather.5.cloned.1.call-done = bf16[1536,1792]{1,0:T(8,128)(2,1)} async-done(((bf16[192,1792]{1,0:T(8,128)(2,1)}), bf16[1536,1792]{1,0:T(8,128)(2,1)}) %all-gather.5.cloned.1.call-update) | async-done | bytes 5505040 | tf_op jit(solution)/shard_map/all_gather | solution.py:90
  99.0 19.8 %conditional.1 = (bf16[2,1792,1024]{1,2,0:T(8,128)(2,1)}) conditional(s32[]{:T(128)} %convert_element_type.50, (s32[1536]{0:T(1024)S(1)}, bf16[1536,1024]{1,0:T(8,128)(2,1)}, bf16[1536,1792]{1,0:T(8,128)(2,1)}) %tuple.11, (bf16[1536,1792]{1,0:T(8,128)(2,1)}, bf16[1536,1024]{1,0:T(8,128)(2,1)}, s32[]{:T(128)}) %tuple.12), branch_computations={%region_2.3_spmd, %region_3.4_spmd} | conditional | flops 11281106944 | bytes 73935424 | solution.py:65
  99.0 9.5 %convolution_bitcast_fusion = bf16[1,1792,1024]{1,2,0:T(8,128)(2,1)S(1)} fusion(bf16[1536,1792]{1,0:T(8,128)(2,1)} %get-tuple-element.22, bf16[1536,1024]{1,0:T(8,128)(2,1)} %get-tuple-element.21, pred[1536]{0:T(1024)(128)(4,1)S(1)} %broadcast_compare_fusion), kind=kOutput, calls=%fused_computation.1 | convolution fusion | flops 5638717440 | bytes 12322304 | tf_op jit(solution)/shard_map/cond/branch_0_fun/dot_general | solution.py:43
  108.5 6.6 %convolution_bitcast_fusion.1 = bf16[1,1792,1024]{1,2,0:T(8,128)(2,1)S(1)} fusion(bf16[1536,1792]{1,0:T(8,128)(2,1)S(1)} %copy-done, bf16[1536,1024]{1,0:T(8,128)(2,1)S(1)} %copy-done.2, pred[1536]{0:T(1024)(128)(4,1)S(1)} %broadcast_compare_fusion), kind=kOutput, calls=%fused_computation.2 | convolution fusion | flops 5638717440 | bytes 12322304 | tf_op jit(solution)/shard_map/cond/branch_0_fun/dot_general | solution.py:43
  115.1 3.6 %pad_maximum_fusion = bf16[2,1792,1024]{1,2,0:T(8,128)(2,1)} fusion(bf16[1,1792,1024]{1,2,0:T(8,128)(2,1)S(1)} %convolution_bitcast_fusion, bf16[1,1792,1024]{1,2,0:T(8,128)(2,1)S(1)} %convolution_bitcast_fusion.1), kind=kLoop, calls=%fused_computation | loop fusion | flops 3670016 | bytes 14680064 | tf_op jit(solution)/shard_map/cond/branch_0_fun/stack | solution.py:63
  118.7 4.7 %fusion.11 = (f32[]{:T(128)}, f32[]{:T(128)}) fusion(bf16[2,1792,1024]{1,2,0:T(8,128)(2,1)} %get-tuple-element.38), kind=kLoop, calls=%fused_computation.22 | loop fusion | flops 11010046 | bytes 7340040 | tf_op jit(solution)/shard_map/reduce_sum | solution.py:96
  123.4 9.4 %all-reduce.2 = (f32[]{:T(128)}, f32[]{:T(128)}) all-reduce(f32[]{:T(128)} %get-tuple-element.27, f32[]{:T(128)} %get-tuple-element.26), channel_id=1, replica_groups=mesh['row_0'=4,'row_1'=4,'col_0'=4,'col_1'=2] {'row_0'}, use_global_device_ids=true, to_apply=%region_10.11 | all-reduce | flops 2 | bytes 16 | tf_op jit(solution)/shard_map/psum | solution.py:25
  132.8 9.0 %all-reduce.1 = (f32[]{:T(128)}, f32[]{:T(128)}) all-reduce(f32[]{:T(128)} %get-tuple-element.32, f32[]{:T(128)} %get-tuple-element.33), channel_id=1, replica_groups=mesh['row_0'=4,'row_1'=4,'col_0'=4,'col_1'=2] {'row_1'}, use_global_device_ids=true, to_apply=%region_11.12 | all-reduce | flops 2 | bytes 16 | tf_op jit(solution)/shard_map/psum | solution.py:25
  141.8 7.4 %all-reduce = (f32[]{:T(128)}, f32[]{:T(128)}) all-reduce(f32[]{:T(128)} %get-tuple-element.30, f32[]{:T(128)} %get-tuple-element.31), channel_id=1, replica_groups=mesh['row_0'=4,'row_1'=4,'col_0'=4,'col_1'=2] {'col_0'}, use_global_device_ids=true, to_apply=%region_12.13 | all-reduce | flops 2 | bytes 16 | tf_op jit(solution)/shard_map/psum | solution.py:25
  149.2 9.1 %all-reduce.3 = (f32[]{:T(128)}, f32[]{:T(128)}) all-reduce(f32[]{:T(128)} %get-tuple-element.28, f32[]{:T(128)} %get-tuple-element.29), channel_id=1, replica_groups=mesh['row_0'=4,'row_1'=4,'col_0'=4,'col_1'=2] {'col_1'}, use_global_device_ids=true, to_apply=%region_13.14 | all-reduce | flops 2 | bytes 16 | tf_op jit(solution)/shard_map/psum | solution.py:25
  159.6 3.8 %fusion.13 = bf16[1,1792,1024]{1,2,0:T(8,128)(2,1)S(1)} fusion(f32[]{:T(128)S(6)} %div.29, f32[]{:T(128)S(6)} %div.28, bf16[2,1792,1024]{1,2,0:T(8,128)(2,1)} %get-tuple-element.38), kind=kLoop, calls=%fused_computation.24 | loop fusion | flops 11010048 | bytes 11010056 | tf_op jit(solution)/shard_map/convert_element_type | solution.py:106
  165.0 3.8 %fusion.54 = bf16[1792,1024]{0,1:T(8,128)(2,1)S(1)} fusion(bf16[2,1792,1024]{1,2,0:T(8,128)(2,1)} %get-tuple-element.38, f32[]{:T(128)S(6)} %div.29, f32[]{:T(128)S(6)} %div.28), kind=kLoop, calls=%fused_computation.62 | loop fusion | flops 11010048 | bytes 11010056 | tf_op jit(solution)/shard_map/convert_element_type | solution.py:106
  168.9 43.7 %collective-permute-done = bf16[1024,1024]{0,1:T(8,128)(2,1)} collective-permute-done((bf16[1024,1024]{0,1:T(8,128)(2,1)S(1)}, bf16[1024,1024]{0,1:T(8,128)(2,1)}, u32[]{:S(2)}, u32[]{:S(2)}) %collective-permute-start) | collective-permute-done | bytes 2097184 | tf_op jit(solution)/shard_map/ppermute | solution.py:32
  212.6 6.1 %fusion.34 = (bf16[1024,1024]{0,1:T(8,128)(2,1)}, bf16[1024,1024]{0,1:T(8,128)(2,1)S(1)}) fusion(s32[]{:T(128)S(6)} %select_n.65, bf16[1792,1024]{0,1:T(8,128)(2,1)S(1)} %fusion.54, bf16[1024,1024]{0,1:T(8,128)(2,1)} %collective-permute-done, s32[]{:T(128)S(6)} %select_n.66), kind=kLoop, calls=%fused_computation.43 | loop fusion | flops 8388608 | bytes 9961480 | tf_op jit(solution)/shard_map/concatenate | solution.py:108
  218.6 3.9 %copy.9 = bf16[1024,1024]{1,0:T(8,128)(2,1)} copy(bf16[1024,1024]{0,1:T(8,128)(2,1)} %get-tuple-element.36) | data formatting | bytes 4194304 | tf_op jit(solution)/shard_map/dynamic_slice | solution.py:122
  222.6 2.5 copy.10
  225.1 17.2 %fusion.10 = bf16[2,1024,1,1024]{3,1,0,2:T(8,128)(2,1)} fusion(bf16[1,1024,1,1024]{3,1,0,2:T(8,128)(2,1)} %bitcast.67, bf16[1,1024,1,1024]{3,1,0,2:T(8,128)(2,1)} %bitcast.66), kind=kOutput, calls=%fused_computation.21 | convolution fusion | flops 8619294720 | bytes 8388608 | tf_op jit(solution)/shard_map/sbik,skbj->sibj/dot_general | solution.py:74
  242.3 17.0 %fusion.9 = bf16[2,1024,1,1024]{3,1,0,2:T(8,128)(2,1)} fusion(bf16[2,1024,1,1024]{3,1,0,2:T(8,128)(2,1)} %fusion.10), kind=kOutput, calls=%fused_computation.19 | convolution fusion | flops 8604614656 | bytes 8388608 | tf_op jit(solution)/shard_map/sbik,skbj->sibj/dot_general | solution.py:74
  261.0 3.2 broadcast_in_dim.47
  264.2 10.5 %dynamic_update_slice.10 = bf16[2816,1024]{1,0:T(8,128)(2,1)} dynamic-update-slice(bf16[2816,1024]{1,0:T(8,128)(2,1)} %broadcast_in_dim.47, bf16[1024,1024]{1,0:T(8,128)(2,1)S(1)} %fusion.36, s32[]{:T(128)S(6)} %select_n.65, s32[]{:T(128)} %constant.63.clone.1) | dynamic-update-slice | bytes 4194308 | tf_op jit(solution)/shard_map/dynamic_update_slice | solution.py:129
  274.8 3.2 fusion.35
  278.0 10.6 %dynamic_update_slice.11 = bf16[2816,1024]{1,0:T(8,128)(2,1)} dynamic-update-slice(bf16[2816,1024]{1,0:T(8,128)(2,1)} %dynamic_update_slice.10, bf16[1024,1024]{1,0:T(8,128)(2,1)S(1)} %fusion.35, s32[]{:T(128)S(6)} %select_n.66, s32[]{:T(128)} %constant.63.clone.1) | dynamic-update-slice | bytes 4194308 | tf_op jit(solution)/shard_map/dynamic_update_slice | solution.py:129
  293.4 42.1 %collective-permute-done.1 = bf16[1024,1024]{1,0:T(8,128)(2,1)S(1)} collective-permute-done((bf16[1024,1024]{1,0:T(8,128)(2,1)S(1)}, bf16[1024,1024]{1,0:T(8,128)(2,1)S(1)}, u32[]{:S(2)}, u32[]{:S(2)}) %collective-permute-start.1) | collective-permute-done | bytes 2097184 | tf_op jit(solution)/shard_map/ppermute | solution.py:32
  (22 shorter events, 16.2 us)
Async XLA Ops:
  6.5 53.5 %all-gather.3.cloned.1.call-start = ((), (), s32[]{:S(2)}) async-start(), calls=%async_computation | async-start | bytes 3342336 | tf_op jit(solution)/shard_map/all_gather | solution.py:88
  7.3 91.7 %all-gather.5.cloned.1.call-start = ((), (), s32[]{:S(2)}) async-start(), calls=%async_computation.1 | async-start | bytes 6193152 | tf_op jit(solution)/shard_map/all_gather | solution.py:90
  99.0 9.6 %copy-start = (bf16[1536,1792]{1,0:T(8,128)(2,1)S(1)}, bf16[1536,1792]{1,0:T(8,128)(2,1)}, u32[]{:S(2)}) copy-start(bf16[1536,1792]{1,0:T(8,128)(2,1)} %get-tuple-element.22) | copy-start | bytes 16515076 | tf_op jit(solution)/shard_map/cond
  99.0 9.6 %copy-start.2 = (bf16[1536,1024]{1,0:T(8,128)(2,1)S(1)}, bf16[1536,1024]{1,0:T(8,128)(2,1)}, u32[]{:S(2)}) copy-start(bf16[1536,1024]{1,0:T(8,128)(2,1)} %get-tuple-element.21) | copy-start | bytes 9437188 | tf_op jit(solution)/shard_map/cond
  163.7 48.8 %collective-permute-start = (bf16[1024,1024]{0,1:T(8,128)(2,1)S(1)}, bf16[1024,1024]{0,1:T(8,128)(2,1)}, u32[]{:S(2)}, u32[]{:S(2)}) collective-permute-start(bf16[1024,1024]{0,1:T(8,128)(2,1)S(1)} %slice_bitcast_fusion.1), channel_id=1, source_target_pairs={{8,0},{16,8},{24,16},{32,24},{40,32},{48,40},{56,48},{64,56},{72,6... | collective-permute-start | bytes 6291464 | tf_op jit(solution)/shard_map/ppermute | solution.py:32
  290.3 45.1 %collective-permute-start.1 = (bf16[1024,1024]{1,0:T(8,128)(2,1)S(1)}, bf16[1024,1024]{1,0:T(8,128)(2,1)S(1)}, u32[]{:S(2)}, u32[]{:S(2)}) collective-permute-start(bf16[1024,1024]{1,0:T(8,128)(2,1)S(1)} %slice.46), channel_id=1, source_target_pairs={{0,8},{8,16},{16,24},{24,32},{32,40},{40,48},{48,56},{56,64},{64,7... | collective-permute-start | bytes 6291464 | tf_op jit(solution)/shard_map/ppermute | solution.py:32
Sparse Core Ops, SparseCore 0:
  9.5 50.4 all-gather.2
  61.7 37.2 all-gather.4
where the time goes:
time: 350 us; the launch traced here: 346 us
  waiting for transfers between devices  175 us (50%)
  matrix products  50.3 us (14%)
  local copies, waits for them, and re-layouts  34.9 us (10%)
  blocking collectives  34.8 us (10%)
  other arithmetic  33.3 us (10%)
  between operations  15.5 us (4%)
    ppermute x2, waiting for transfers between devices, shifted(): return lax.ppermute(value, axis, pairs)  85.7 us
    all_gather x1, waiting for transfers between devices, per_device(): grads_whole = lax.all_gather(out_grads, ROW, axis=0, tiled=True)  48.7 us
    all_gather x1, waiting for transfers between devices, per_device(): lax.all_gather(inputs, COL, axis=0, tiled=True)  39 us
    psum x4, blocking collectives, one_axis_at_a_time(): value = lax.psum(value, axis)  34.8 us
    dot_general x2, matrix products, newton(): jnp.einsum('sbik,skbj->sibj', gram_matrix, iterate, preferred_element_typ...  34.2 us
    dynamic_update_slice x2, local copies, waits for them, and re-layouts, per_device(): lax.dynamic_update_slice_in_dim(placed, jnp.where(slot_valid[slot], fresh...  21.1 us
    dot_general x2, matrix products, contract(): lax.dot_general(input_rows, grad_rows, (((0,), (0,)), ((), ())), preferre...  16.1 us
    convert_element_type x2, other arithmetic, per_device(): update = blended.astype(jnp.bfloat16)  7.69 us
  transfers between devices with their start and end apart: 4, of which 4 were waited for; matrix products, arithmetic and copies ran while one was open for 2% of the time, Pallas kernels for 0%

commit v1 on v0

v1 whole, which is shorter than its diff:
```python
import math

import jax
import jax.numpy as jnp
from jax import lax
from jax.experimental import pallas as pl
from jax.experimental.pallas import tpu as pltpu
from jax.sharding import Mesh
from jax.sharding import PartitionSpec as P

FF = 28672
D = 8192
BLOCK = 1024
TARGET = 0.15 * math.sqrt(FF * D / BLOCK)
LAST_SCALE = math.sqrt(BLOCK)

MESH = pl.DeviceIdType.MESH
CH = 256
OWN = 7
SLAB = 192
MB = 384
GS = 96
HALF = 512
MINUS, PLUS = 0, 1


def dot_tn(a, b):
    return lax.dot_general(a, b, (((0,), (0,)), ((), ())), preferred_element_type=jnp.float32)


def dot_nt(a, b):
    return lax.dot_general(a, b, (((1,), (1,)), ((), ())), preferred_element_type=jnp.float32)


def dot_nn(a, b):
    return lax.dot_general(a, b, (((1,), (0,)), ((), ())), preferred_element_type=jnp.float32)


def kernel(
    uids, inp, og, out,
    IN, OG, ACC, G, X, X1, A, OUTB, SQ, S1, R1, S2, R2,
    sy, ry, sf, rf, sb, rb, lc, sx, rx,
    oa1s, oa1r, of1s, of1r, oa2s, oa2r, of2s, of2r, ol,
    a1s, a1r, a2s, a2r, ret_s, ret_r, od,
):
    z, x, y, c = (lax.axis_index(a) for a in ("z", "x", "y", "c"))
    zm, zp, zf = (lax.rem(z + d, 4) for d in (3, 1, 2))
    xm, xp, xf = (lax.rem(x + d, 4) for d in (3, 1, 2))
    ym, yp, yf = (lax.rem(y + d, 4) for d in (3, 1, 2))
    sib = 1 - c
    inner = jnp.logical_or(x == 1, x == 2)
    nch = jnp.where(inner, OWN + 2, OWN + 1)
    col = y * 2 + c
    row = z * 4 + x

    barrier = pltpu.get_barrier_semaphore()

    def greet_col(d, _):
        p = lax.rem(col + d, 8)
        pl.semaphore_signal(barrier, inc=1, device_id=(z, x, lax.div(p, 2), lax.rem(p, 2)), device_id_type=MESH)
        return 0

    def greet_row(d, _):
        p = lax.rem(row + d, 16)
        pl.semaphore_signal(barrier, inc=1, device_id=(lax.div(p, 4), lax.rem(p, 4), y, c), device_id_type=MESH)
        return 0

    lax.fori_loop(1, 8, greet_col, 0)
    lax.fori_loop(1, 16, greet_row, 0)
    pl.semaphore_wait(barrier, 22)

    def remote(src, dst, ss, rs, dev):
        return pltpu.make_async_remote_copy(
            src_ref=src, dst_ref=dst, send_sem=ss, recv_sem=rs, device_id=dev, device_id_type=MESH
        )

    ydev = [(z, x, ym, c), (z, x, yp, c)]
    xdev = [(z, xm, y, c), (z, xp, y, c)]
    zdev = [(zm, x, y, c), (zp, x, y, c)]
    sdev = (z, x, y, sib)

    def rows_of(yy, cc):
        return pl.ds(pl.multiple_of((yy * 2 + cc) * SLAB, SLAB), SLAB)

    mine = rows_of(y, c)

    def extra(src_chunk, slot, direction, k):
        return remote(
            inp.at[:, pl.ds(src_chunk * CH, CH)], IN.at[OWN + slot, mine], sx.at[k], rx.at[slot], xdev[direction]
        )

    @pl.when(x == 1)
    def _():
        extra(0, 0, MINUS, 0).start()
        extra(5, 0, PLUS, 1).start()
        extra(6, 1, PLUS, 2).start()

    @pl.when(x == 2)
    def _():
        extra(6, 0, PLUS, 0).start()
        extra(0, 0, MINUS, 1).start()
        extra(1, 1, MINUS, 2).start()

    def grow(zz, xx):
        return pl.ds(pl.multiple_of((zz * 4 + xx) * GS, GS), GS)

    def gpart(zz, xx, part):
        return pl.ds(pl.multiple_of((zz * 4 + xx) * GS + part * (GS // 2), GS // 2), GS // 2)

    first_dev = [xdev, zdev]
    second_dev = [zdev, xdev]

    def along_first(h, d):
        if h == 0:
            return (z, [x, xm, xp, xf][d])
        return ([z, zm, zp, zf][d], x)

    def second_of(h, slot, d):
        zz, xx = along_first(h, slot)
        if h == 0:
            return ([z, zm, zp, zf][d], xx)
        return (zz, [x, xm, xp, xf][d])

    def first_send(h, direction):
        r = grow(z, x)
        return remote(
            og.at[:, pl.ds(h * HALF, HALF)], OG.at[h, r], oa1s.at[h, direction], oa1r.at[h, 1 - direction],
            first_dev[h][direction],
        )

    def first_wait(h, frm):
        r = grow(*along_first(h, 1 + frm))
        remote(OG.at[h, r], OG.at[h, r], oa1s.at[h, frm], oa1r.at[h, frm], first_dev[h][frm]).wait_recv()

    def first_forward(h, frm):
        r = gpart(*along_first(h, 1 + frm), frm)
        return remote(
            OG.at[h, r], OG.at[h, r], of1s.at[h, frm], of1r.at[h, frm], first_dev[h][1 - frm]
        )

    def first_far_wait(h, frm):
        r = gpart(*along_first(h, 3), frm)
        remote(OG.at[h, r], OG.at[h, r], of1s.at[h, frm], of1r.at[h, frm], first_dev[h][frm]).wait_recv()

    def second_send(h, slot, direction):
        r = grow(*along_first(h, slot))
        src = og.at[:, pl.ds(h * HALF, HALF)] if slot == 0 else OG.at[h, r]
        return remote(
            src, OG.at[h, r], oa2s.at[h, slot, direction], oa2r.at[h, slot, 1 - direction], second_dev[h][direction]
        )

    def second_wait(h, slot, frm):
        r = grow(*second_of(h, slot, 1 + frm))
        remote(
            OG.at[h, r], OG.at[h, r], oa2s.at[h, slot, frm], oa2r.at[h, slot, frm], second_dev[h][frm]
        ).wait_recv()

    def second_forward(h, slot, frm):
        r = gpart(*second_of(h, slot, 1 + frm), frm)
        return remote(
            OG.at[h, r], OG.at[h, r], of2s.at[h, slot, frm], of2r.at[h, slot, frm], second_dev[h][1 - frm]
        )

    def second_far_wait(h, slot, frm):
        r = gpart(*second_of(h, slot, 3), frm)
        remote(
            OG.at[h, r], OG.at[h, r], of2s.at[h, slot, frm], of2r.at[h, slot, frm], second_dev[h][frm]
        ).wait_recv()

    for h in (0, 1):
        for d in (MINUS, PLUS):
            first_send(h, d).start()
    for h in (0, 1):
        for d in (MINUS, PLUS):
            second_send(h, 0, d).start()

    def own_src(k):
        return inp.at[:, pl.ds(pl.multiple_of(k * CH, CH), CH)]

    def y_send(src, k, direction):
        return remote(src, IN.at[k, mine], sy.at[direction, k], ry.at[1 - direction, k], ydev[direction])

    def relay(src, kind, k, yy):
        return remote(src, IN.at[k, rows_of(yy, c)], sb.at[kind, k], rb.at[kind, k], sdev)

    def local(k):
        return pltpu.make_async_copy(own_src(k), IN.at[k, mine], lc.at[k])

    def start_own(k, _):
        y_send(own_src(k), k, MINUS).start()
        y_send(own_src(k), k, PLUS).start()
        return 0

    lax.fori_loop(0, OWN, start_own, 0)

    def start_near(k, _):
        local(k).start()
        relay(own_src(k), 0, k, y).start()
        return 0

    lax.fori_loop(0, OWN, start_near, 0)

    def og_local(h):
        return pltpu.make_async_copy(og.at[:, pl.ds(h * HALF, HALF)], OG.at[h, grow(z, x)], ol.at[h])

    og_local(0).start()
    og_local(1).start()

    def start_extra(k, _):
        slot = k - OWN
        src = IN.at[k, mine]
        remote(src, src, sx.at[0], rx.at[slot], xdev[0]).wait_recv()
        y_send(src, k, MINUS).start()
        y_send(src, k, PLUS).start()
        relay(src, 0, k, y).start()
        return 0

    lax.fori_loop(OWN, nch, start_extra, 0)

    for h in (1, 0):
        for frm in (MINUS, PLUS):
            first_wait(h, frm)
            first_forward(h, frm).start()
            for d in (MINUS, PLUS):
                second_send(h, 1 + frm, d).start()
    for h in (1, 0):
        for frm in (MINUS, PLUS):
            second_wait(h, 0, frm)
            second_forward(h, 0, frm).start()
    for h in (1, 0):
        for frm in (MINUS, PLUS):
            first_far_wait(h, frm)
        for d in (MINUS, PLUS):
            second_send(h, 3, d).start()
    for slot in (1, 2, 3):
        for h in (1, 0):
            for frm in (MINUS, PLUS):
                second_wait(h, slot, frm)
                second_forward(h, slot, frm).start()

    def y_wait(k, frm):
        r = IN.at[k, rows_of([ym, yp][frm], c)]
        remote(r, r, sy.at[frm, k], ry.at[frm, k], ydev[frm]).wait_recv()

    def y_forward(k, frm):
        r = IN.at[k, rows_of([ym, yp][frm], c)]
        return remote(r, r, sf.at[k], rf.at[k], ydev[1 - frm])

    def y_far_wait(k):
        r = IN.at[k, rows_of(yf, c)]
        remote(r, r, sf.at[k], rf.at[k], ydev[0]).wait_recv()

    def relay_wait(kind, k, yy):
        r = IN.at[k, rows_of(yy, sib)]
        remote(r, r, sb.at[kind, k], rb.at[kind, k], sdev).wait_recv()

    def middle(k, _):
        for frm in (MINUS, PLUS):
            y_wait(k, frm)

            @pl.when(lax.rem(k, 2) == frm)
            def _():
                y_forward(k, frm).start()

            relay(IN.at[k, rows_of([ym, yp][frm], c)], 1 + frm, k, [ym, yp][frm]).start()
        return 0

    lax.fori_loop(0, nch, middle, 0)

    for slot in (0, 1, 2, 3):
        for h in (1, 0):
            for frm in (MINUS, PLUS):
                second_far_wait(h, slot, frm)
    og_local(0).wait()
    og_local(1).wait()

    def local_wait(k, _):
        local(k).wait()
        return 0

    lax.fori_loop(0, OWN, local_wait, 0)

    def weight(m):
        one = uids[m].astype(jnp.float32)
        return 1.0 - one, one

    def mb_rows(m):
        return pl.ds(pl.multiple_of(m * MB, MB), MB)

    near = [y, ym, yp]
    near_w = [weight(m) for m in near]

    def near_grads(k, _):
        relay_wait(0, k, y)
        relay_wait(1, k, ym)
        relay_wait(2, k, yp)
        for h in (0, 1):
            cols = slice(h * HALF, (h + 1) * HALF)
            zero = one = None
            for m, (w0, w1) in zip(near, near_w):
                p = dot_tn(IN[k, mb_rows(m)], OG[h, mb_rows(m)])
                zero = p * w0 if zero is None else zero + p * w0
                one = p * w1 if one is None else one + p * w1
            ACC[k, 0, :, cols] = zero
            ACC[k, 1, :, cols] = one
        return 0

    lax.fori_loop(0, nch, near_grads, 0)

    far_w = weight(yf)
    SQ[...] = jnp.zeros_like(SQ)

    def far_grads(k):
        relay_wait(3, k, yf)
        counts = jnp.where(k < OWN, 1.0, 0.0)
        for h in (0, 1):
            cols = slice(h * HALF, (h + 1) * HALF)
            p = dot_tn(IN[k, mb_rows(yf)], OG[h, mb_rows(yf)])
            for u in (0, 1):
                g = (ACC[k, u, :, cols] + p * far_w[u]).astype(jnp.bfloat16)
                G[k, u, :, cols] = g
                wide = g.astype(jnp.float32)
                SQ[u : u + 1, cols] += jnp.sum(wide * wide, axis=0, keepdims=True) * counts

    def far(k, _):
        y_far_wait(k)
        relay(IN.at[k, rows_of(yf, c)], 3, k, yf).start()

        @pl.when(k > 0)
        def _():
            far_grads(k - 1)

        return 0

    lax.fori_loop(0, nch, far, 0)
    far_grads(nch - 1)

    sums = jnp.zeros((8, 128), jnp.float32)
    for j in range(8):
        sums = sums + SQ[:, j * 128 : (j + 1) * 128]
    S1[...] = sums

    def col_copy(d):
        p = lax.rem(col + d, 8)
        return remote(S1, R1.at[col], a1s.at[d], a1r.at[col], (z, x, lax.div(p, 2), lax.rem(p, 2)))

    def col_start(d, _):
        col_copy(d).start()
        return 0

    def col_wait(d, _):
        p = lax.rem(col + d, 8)
        remote(S1, R1.at[p], a1s.at[d], a1r.at[p], sdev).wait_recv()
        return 0

    lax.fori_loop(1, 8, col_start, 0)
    R1[col] = S1[...]
    lax.fori_loop(1, 8, col_wait, 0)
    total = R1[0]
    for j in range(1, 8):
        total = total + R1[j]
    S2[...] = total

    def row_copy(d):
        p = lax.rem(row + d, 16)
        return remote(S2, R2.at[row], a2s.at[d], a2r.at[row], (lax.div(p, 4), lax.rem(p, 4), y, c))

    def row_start(d, _):
        row_copy(d).start()
        return 0

    def row_wait(d, _):
        p = lax.rem(row + d, 16)
        remote(S2, R2.at[p], a2s.at[d], a2r.at[p], sdev).wait_recv()
        return 0

    lax.fori_loop(1, 16, row_start, 0)
    R2[row] = S2[...]
    lax.fori_loop(1, 16, row_wait, 0)
    total = R2[0]
    for j in range(1, 16):
        total = total + R2[j]
    factor = TARGET / jnp.sqrt(jnp.sum(total, axis=1, keepdims=True) + 1e-06)
    f0 = factor[0:1, :]
    f1 = factor[1:2, :]

    right = x >= 2
    s1 = jnp.where(inner, 8, jnp.where(right, 0, 4))
    s2 = jnp.where(right, jnp.where(inner, 0, 1), 5)
    shared = [jnp.int32(7), s1, s2, s2 + 1]

    def out_copy(t, i, q):
        return pltpu.make_async_copy(
            OUTB.at[t * 4 + i], out.at[pl.ds(pl.multiple_of(q * CH, CH), CH)], od.at[t * 4 + i]
        )

    def give_back(direction):
        q = 0 if direction == PLUS else OWN - 1
        return remote(OUTB.at[0], out.at[pl.ds(q * CH, CH)], ret_s, ret_r, xdev[direction])

    def chunk_of(t, i):
        return jnp.where(t == 0, shared[i], x + i)

    def task(t, _):
        for i in range(4):
            q = chunk_of(t, i)
            X[i * CH : (i + 1) * CH] = (
                f0 * G[q, 0].astype(jnp.float32) + f1 * G[q, 1].astype(jnp.float32)
            ).astype(jnp.bfloat16)
        for i in range(4):
            r = slice(i * CH, (i + 1) * CH)
            A[r] = dot_nt(X[r], X[...]).astype(jnp.bfloat16)
        for i in range(4):
            r = slice(i * CH, (i + 1) * CH)
            X1[r] = (1.5 * X[r].astype(jnp.float32) - 0.5 * dot_nn(A[r], X[...])).astype(jnp.bfloat16)

        def last(i):
            r = slice(i * CH, (i + 1) * CH)
            gram = dot_nt(X1[r], X1[...]).astype(jnp.bfloat16)
            done = (1.5 * X1[r].astype(jnp.float32) - 0.5 * dot_nn(gram, X1[...])) * LAST_SCALE
            OUTB[t * 4 + i] = done.astype(jnp.bfloat16)

        outer_or_whole = jnp.logical_or(t == 1, jnp.logical_not(inner))

        @pl.when(outer_or_whole)
        def _():
            last(0)

        @pl.when(jnp.logical_and(t == 0, x == 0))
        def _():
            give_back(PLUS).start()

        @pl.when(jnp.logical_and(t == 0, x == 3))
        def _():
            give_back(MINUS).start()

        @pl.when(t == 1)
        def _():
            out_copy(t, 0, chunk_of(t, 0)).start()

        @pl.when(outer_or_whole)
        def _():
            last(1)
            out_copy(t, 1, chunk_of(t, 1)).start()

        for i in (2, 3):
            last(i)
            out_copy(t, i, chunk_of(t, i)).start()
        return 0

    lax.fori_loop(0, 2, task, 0)

    for t in (0, 1):
        for i in range(4):
            if t == 0 and i == 0:
                continue
            if t == 0 and i == 1:

                @pl.when(jnp.logical_not(inner))
                def _():
                    out_copy(0, 1, chunk_of(0, 1)).wait()

                continue
            out_copy(t, i, chunk_of(t, i)).wait()

    @pl.when(x == 0)
    def _():
        give_back(PLUS).wait_send()

    @pl.when(x == 3)
    def _():
        give_back(MINUS).wait_send()

    @pl.when(x == 1)
    def _():
        give_back(PLUS).wait_recv()

    @pl.when(x == 2)
    def _():
        give_back(MINUS).wait_recv()

    @pl.when(inner)
    def _():
        for k in range(3):
            extra(0, 0, MINUS, k).wait_send()

    for h in (0, 1):
        for d in (MINUS, PLUS):
            first_send(h, d).wait_send()
            first_forward(h, d).wait_send()
            for slot in range(4):
                second_send(h, slot, d).wait_send()
                second_forward(h, slot, d).wait_send()

    def drain(k, _):
        src = IN.at[k, mine]
        y_send(src, k, MINUS).wait_send()
        y_send(src, k, PLUS).wait_send()
        y_forward(k, MINUS).wait_send()
        for kind in range(4):
            relay(src, kind, k, y).wait_send()
        return 0

    lax.fori_loop(0, nch, drain, 0)

    def drain_col(d, _):
        col_copy(d).wait_send()
        return 0

    def drain_row(d, _):
        row_copy(d).wait_send()
        return 0

    lax.fori_loop(1, 8, drain_col, 0)
    lax.fori_loop(1, 16, drain_row, 0)


def per_device(inputs, out_grads, user_ids):
    dma = pltpu.SemaphoreType.DMA
    n = OWN + 2
    bf16, f32 = jnp.bfloat16, jnp.float32
    return pl.pallas_call(
        kernel,
        out_shape=jax.ShapeDtypeStruct((OWN * CH, BLOCK), bf16),
        in_specs=[
            pl.BlockSpec(memory_space=pltpu.SMEM),
            pl.BlockSpec(memory_space=pl.ANY),
            pl.BlockSpec(memory_space=pl.ANY),
        ],
        out_specs=pl.BlockSpec(memory_space=pl.ANY),
        scratch_shapes=[
            pltpu.VMEM((n, 4 * MB, CH), bf16),
            pltpu.VMEM((2, 4 * MB, HALF), bf16),
            pltpu.VMEM((n, 2, CH, BLOCK), f32),
            pltpu.VMEM((n, 2, CH, BLOCK), bf16),
            pltpu.VMEM((BLOCK, BLOCK), bf16),
            pltpu.VMEM((BLOCK, BLOCK), bf16),
            pltpu.VMEM((BLOCK, BLOCK), bf16),
            pltpu.VMEM((8, CH, BLOCK), bf16),
            pltpu.VMEM((8, BLOCK), f32),
            pltpu.VMEM((8, 128), f32),
            pltpu.VMEM((8, 8, 128), f32),
            pltpu.VMEM((8, 128), f32),
            pltpu.VMEM((16, 8, 128), f32),
            dma((2, n)), dma((2, n)), dma((n,)), dma((n,)), dma((4, n)), dma((4, n)), dma((n,)), dma((3,)), dma((2,)),
            dma((2, 2)), dma((2, 2)), dma((2, 2)), dma((2, 2)),
            dma((2, 4, 2)), dma((2, 4, 2)), dma((2, 4, 2)), dma((2, 4, 2)), dma((2,)),
            dma((8,)), dma((8,)), dma((16,)), dma((16,)), dma, dma, dma((8,)),
        ],
        compiler_params=pltpu.CompilerParams(
            collective_id=0, has_side_effects=True, vmem_limit_bytes=60 * 1024 * 1024
        ),
    )(user_ids, inputs, out_grads)


def solution(mesh):
    torus = Mesh(mesh.devices.reshape(4, 4, 4, 2), ("z", "x", "y", "c"))
    return jax.shard_map(
        per_device,
        mesh=torus,
        in_specs=(P(("y", "c"), ("z", "x")), P(("z", "x"), ("y", "c")), P()),
        out_specs=P(("z", "x"), ("y", "c")),
        check_vma=False,
    )
```

time: 350 us -> 88.4 us (0.25)
  waiting for transfers between devices: 175 us -> 0 us
  Pallas kernels: 0 us -> 84 us
  matrix products: 50.3 us -> 0 us
  blocking collectives: 34.8 us -> 0 us
  other arithmetic: 33.3 us -> 0 us
  local copies, waits for them, and re-layouts: 34.9 us -> 4.25 us
  between operations: 15.5 us -> 0.01 us
    all_gather x2 -> x0, waiting for transfers between devices: 87.6 us -> none  [the longest x1 48.7 us: per_device(): grads_whole = lax.all_gather(out_grads, ROW, axis=0, tiled=True)]
    ppermute x2 -> x0, waiting for transfers between devices: 85.7 us -> none  [shifted(): return lax.ppermute(value, axis, pairs)]
    pallas_call x0 -> x1, Pallas kernels: none -> 84 us  [per_device(): pl.pallas_call(kernel, out_shape=jax.ShapeDtypeStruct((OWN * CH, BLOCK),...]
    dot_general x4 -> x0, matrix products: 50.3 us -> none  [the longest x2 34.2 us: newton(): jnp.einsum('sbik,skbj->sibj', gram_matrix, iterate, preferred_element_typ...]
    psum x4 -> x0, blocking collectives: 34.8 us -> none  [one_axis_at_a_time(): value = lax.psum(value, axis)]
    dynamic_update_slice x2 -> x0, local copies, waits for them, and re-layouts: 21.1 us -> none  [per_device(): lax.dynamic_update_slice_in_dim(placed, jnp.where(slot_valid[slot], fresh...]
    concatenate x2 -> x0, other arithmetic: 8.3 us -> none  [the longest x1 6.09 us: per_device(): extended = jnp.concatenate([update, next_head], axis=0)]
    convert_element_type x2 -> x0, other arithmetic: 7.69 us -> none  [per_device(): update = blended.astype(jnp.bfloat16)]
  transfers between devices with their start and end apart: 4 -> 0, of which waited for: 4 -> 0; matrix products, arithmetic and copies ran while one was open for 2% -> 0% of each run, Pallas kernels for 0% -> 0%
where the time goes in v1:
time: 88.4 us; the launch traced here: 88.3 us
  Pallas kernels  84 us (95%)
  local copies, waits for them, and re-layouts  4.25 us (5%)
    pallas_call x1, Pallas kernels, per_device(): pl.pallas_call(kernel, out_shape=jax.ShapeDtypeStruct((OWN * CH, BLOCK),...  84 us
    unnamed x1, local copies, waits for them, and re-layouts  4.25 us

profile of v1, /device:TPU:1, one launch (start us, length us, event | category | flops | bytes accessed | tf_op | source)
XLA Modules:
  0.0 88.3 jit_solution(16655670994757624214)
XLA Ops:
  0.0 84.0 %shard_map.37 = bf16[1792,1024]{1,0:T(8,128)(2,1)} custom-call(s32[4]{0:T(128)} %uids.1, bf16[192,1792]{1,0:T(8,128)(2,1)} %inp.1, bf16[96,1024]{1,0:T(8,128)(2,1)} %og.1), custom_call_target="tpu_custom_call" | custom-call | tf_op jit(solution)/shard_map/pallas_call | solution.py:522
  84.0 4.2 %copy.5 = bf16[1792,1024]{1,0:T(8,128)(2,1)} copy(bf16[1792,1024]{1,0:T(8,128)(2,1)} %shard_map.37) | data formatting | bytes 7340032

commit v2 on v1

v2 whole, which is shorter than its diff:
```python
import math

import jax
import jax.numpy as jnp
from jax import lax
from jax.experimental import pallas as pl
from jax.experimental.pallas import tpu as pltpu
from jax.sharding import Mesh
from jax.sharding import PartitionSpec as P

FF = 28672
D = 8192
BLOCK = 1024
TARGET = 0.15 * math.sqrt(FF * D / BLOCK)
LAST_SCALE = math.sqrt(BLOCK)

MESH = pl.DeviceIdType.MESH
CH = 256
OWN = 7
SLAB = 192
MB = 384
GS = 96
HALF = 512
MINUS, PLUS = 0, 1


def dot_tn(a, b):
    return lax.dot_general(a, b, (((0,), (0,)), ((), ())), preferred_element_type=jnp.float32)


def dot_nt(a, b):
    return lax.dot_general(a, b, (((1,), (1,)), ((), ())), preferred_element_type=jnp.float32)


def dot_nn(a, b):
    return lax.dot_general(a, b, (((1,), (0,)), ((), ())), preferred_element_type=jnp.float32)


def kernel(
    uids, inp, og, out,
    NEAR, FAR, XNEAR, XFAR, OG, G, X, X1, A, BACK, SQ, S1, R1, S2, R2,
    sy, ry, sf, rf, sh, rh, sb, rb, lc, sx, rx,
    oa1s, oa1r, of1s, of1r, oa2s, oa2r, of2s, of2r, ol,
    a1s, a1r, a2s, a2r, ret_s, ret_r,
):
    z, x, y, c = (lax.axis_index(a) for a in ("z", "x", "y", "c"))
    zm, zp, zf = (lax.rem(z + d, 4) for d in (3, 1, 2))
    xm, xp, xf = (lax.rem(x + d, 4) for d in (3, 1, 2))
    ym, yp, yf = (lax.rem(y + d, 4) for d in (3, 1, 2))
    sib = 1 - c
    inner = jnp.logical_or(x == 1, x == 2)
    extras = jnp.where(inner, 2, 1)
    col = y * 2 + c
    row = z * 4 + x

    barrier = pltpu.get_barrier_semaphore()
    for dev in ((z, x, ym, c), (z, x, yp, c), (z, xm, y, c), (z, xp, y, c), (zm, x, y, c), (zp, x, y, c), (z, x, y, sib)):
        pl.semaphore_signal(barrier, inc=1, device_id=dev, device_id_type=MESH)
    pl.semaphore_wait(barrier, 7)

    def remote(src, dst, ss, rs, dev):
        return pltpu.make_async_remote_copy(
            src_ref=src, dst_ref=dst, send_sem=ss, recv_sem=rs, device_id=dev, device_id_type=MESH
        )

    ydev = [(z, x, ym, c), (z, x, yp, c)]
    xdev = [(z, xm, y, c), (z, xp, y, c)]
    zdev = [(zm, x, y, c), (zp, x, y, c)]
    sdev = (z, x, y, sib)

    def slab(cc):
        return pl.ds(pl.multiple_of(cc * SLAB, SLAB), SLAB)

    def extra(src_chunk, slot, direction, k):
        return remote(
            inp.at[:, pl.ds(src_chunk * CH, CH)], XNEAR.at[slot, 0, slab(c)], sx.at[k], rx.at[slot], xdev[direction]
        )

    def start_shared():
        @pl.when(x == 1)
        def _():
            extra(5, 0, PLUS, 0).start()
            extra(0, 0, MINUS, 1).start()
            extra(6, 1, PLUS, 2).start()

        @pl.when(x == 2)
        def _():
            extra(0, 0, MINUS, 0).start()
            extra(6, 0, PLUS, 1).start()
            extra(1, 1, MINUS, 2).start()

    def grow(zz, xx):
        return zz, pl.ds(pl.multiple_of(xx * GS, GS), GS)

    def gpart(zz, xx, part):
        return zz, pl.ds(pl.multiple_of(xx * GS + part * (GS // 2), GS // 2), GS // 2)

    first_dev = [xdev, zdev]
    second_dev = [zdev, xdev]

    def along_first(h, d):
        if h == 0:
            return (z, [x, xm, xp, xf][d])
        return ([z, zm, zp, zf][d], x)

    def second_of(h, slot, d):
        zz, xx = along_first(h, slot)
        if h == 0:
            return ([z, zm, zp, zf][d], xx)
        return (zz, [x, xm, xp, xf][d])

    def first_send(h, direction):
        r = grow(z, x)
        return remote(
            og.at[:, pl.ds(h * HALF, HALF)], OG.at[h, r[0], r[1]], oa1s.at[h, direction], oa1r.at[h, 1 - direction],
            first_dev[h][direction],
        )

    def first_wait(h, frm):
        r = grow(*along_first(h, 1 + frm))
        remote(OG.at[h, r[0], r[1]], OG.at[h, r[0], r[1]], oa1s.at[h, frm], oa1r.at[h, frm], first_dev[h][frm]).wait_recv()

    def first_forward(h, frm):
        r = gpart(*along_first(h, 1 + frm), frm)
        return remote(
            OG.at[h, r[0], r[1]], OG.at[h, r[0], r[1]], of1s.at[h, frm], of1r.at[h, frm], first_dev[h][1 - frm]
        )

    def first_far_wait(h, frm):
        r = gpart(*along_first(h, 3), frm)
        remote(OG.at[h, r[0], r[1]], OG.at[h, r[0], r[1]], of1s.at[h, frm], of1r.at[h, frm], first_dev[h][frm]).wait_recv()

    def second_send(h, slot, direction):
        r = grow(*along_first(h, slot))
        src = og.at[:, pl.ds(h * HALF, HALF)] if slot == 0 else OG.at[h, r[0], r[1]]
        return remote(
            src, OG.at[h, r[0], r[1]], oa2s.at[h, slot, direction], oa2r.at[h, slot, 1 - direction], second_dev[h][direction]
        )

    def second_wait(h, slot, frm):
        r = grow(*second_of(h, slot, 1 + frm))
        remote(
            OG.at[h, r[0], r[1]], OG.at[h, r[0], r[1]], oa2s.at[h, slot, frm], oa2r.at[h, slot, frm], second_dev[h][frm]
        ).wait_recv()

    def second_forward(h, slot, frm):
        r = gpart(*second_of(h, slot, 1 + frm), frm)
        return remote(
            OG.at[h, r[0], r[1]], OG.at[h, r[0], r[1]], of2s.at[h, slot, frm], of2r.at[h, slot, frm], second_dev[h][1 - frm]
        )

    def second_far_wait(h, slot, frm):
        r = gpart(*second_of(h, slot, 3), frm)
        remote(
            OG.at[h, r[0], r[1]], OG.at[h, r[0], r[1]], of2s.at[h, slot, frm], of2r.at[h, slot, frm], second_dev[h][frm]
        ).wait_recv()

    for h in (0, 1):
        for d in (MINUS, PLUS):
            first_send(h, d).start()
    for h in (0, 1):
        for d in (MINUS, PLUS):
            second_send(h, 0, d).start()

    place_of = (2, 1)

    def own_src(k):
        return inp.at[:, pl.ds(pl.multiple_of(k * CH, CH), CH)]

    def y_send(src, buf, k, g, direction):
        return remote(
            src, buf.at[k, place_of[1 - direction], slab(c)], sy.at[direction, g], ry.at[1 - direction, g], ydev[direction]
        )

    def y_wait(buf, k, g, frm):
        r = buf.at[k, place_of[frm], slab(c)]
        remote(r, r, sy.at[frm, g], ry.at[frm, g], ydev[frm]).wait_recv()

    def y_forward(buf, dst, k, g, frm):
        return remote(
            buf.at[k, place_of[frm], slab(c)], dst.at[k, slab(c)], sf.at[g], rf.at[g], ydev[1 - frm]
        )

    def split_forward(frm):
        k = OWN - 1
        part = pl.ds(pl.multiple_of(c * SLAB + frm * (SLAB // 2), SLAB // 2), SLAB // 2)
        return remote(NEAR.at[k, place_of[frm], part], FAR.at[k, part], sh.at[frm], rh.at[frm], ydev[1 - frm])

    def y_far_wait(dst, k, g):
        r = dst.at[k, slab(c)]
        remote(r, r, sf.at[g], rf.at[g], ydev[0]).wait_recv()

    def relay(src, dst, k, g, kind):
        r = slab(c)
        return remote(src, dst.at[k, r] if kind == 3 else dst.at[k, (0, 2, 1)[kind], r], sb.at[kind, g], rb.at[kind, g], sdev)

    def relay_wait(dst, k, g, kind):
        r = slab(sib)
        r = dst.at[k, r] if kind == 3 else dst.at[k, (0, 2, 1)[kind], r]
        remote(r, r, sb.at[kind, g], rb.at[kind, g], sdev).wait_recv()

    def local(k):
        return pltpu.make_async_copy(own_src(k), NEAR.at[k, 0, slab(c)], lc.at[k])

    def start_own(k, _):
        y_send(own_src(k), NEAR, k, k, MINUS).start()
        y_send(own_src(k), NEAR, k, k, PLUS).start()
        return 0

    lax.fori_loop(0, OWN, start_own, 0)

    def og_local(h):
        return pltpu.make_async_copy(og.at[:, pl.ds(h * HALF, HALF)], OG.at[(h, *grow(z, x))], ol.at[h])

    og_local(0).start()
    og_local(1).start()

    def start_near(k, _):
        local(k).start()
        relay(own_src(k), NEAR, k, k, 0).start()
        return 0

    lax.fori_loop(0, OWN, start_near, 0)

    for h in (1, 0):
        for frm in (MINUS, PLUS):
            first_wait(h, frm)
            first_forward(h, frm).start()
            for d in (MINUS, PLUS):
                second_send(h, 1 + frm, d).start()
    for h in (1, 0):
        for frm in (MINUS, PLUS):
            second_wait(h, 0, frm)
            second_forward(h, 0, frm).start()
    for h in (1, 0):
        for frm in (MINUS, PLUS):
            first_far_wait(h, frm)
        for d in (MINUS, PLUS):
            second_send(h, 3, d).start()
    for slot in (1, 2, 3):
        for h in (1, 0):
            for frm in (MINUS, PLUS):
                second_wait(h, slot, frm)
                second_forward(h, slot, frm).start()

    start_shared()

    def middle(k, _):
        for frm in (MINUS, PLUS):
            y_wait(NEAR, k, k, frm)

            @pl.when(jnp.logical_and(lax.rem(k, 2) == frm, k < OWN - 1))
            def _():
                y_forward(NEAR, FAR, k, k, frm).start()

            relay(NEAR.at[k, place_of[frm], slab(c)], NEAR, k, k, 1 + frm).start()
        return 0

    lax.fori_loop(0, OWN, middle, 0)
    split_forward(MINUS).start()
    split_forward(PLUS).start()

    for slot in (0, 1, 2, 3):
        for h in (1, 0):
            for frm in (MINUS, PLUS):
                second_far_wait(h, slot, frm)
    og_local(0).wait()
    og_local(1).wait()

    def near_wait(k, _):
        local(k).wait()
        for kind in (0, 1, 2):
            relay_wait(NEAR, k, k, kind)
        return 0

    lax.fori_loop(0, OWN, near_wait, 0)

    user_far = uids[yf]
    d1 = lax.rem(uids[yp] + user_far, 2)
    d2 = lax.rem(uids[ym] + user_far, 2)
    near_hit = (1 - d1) + 2 * d1 * (1 - d2)
    near_a = 1 - jnp.minimum(near_hit, 1)
    near_b = 2 - lax.div(near_hit, 2)

    def og_mb(place):
        return lax.rem(y + place + lax.div(place, 2), 4)

    mb_hit, mb_a, mb_b = og_mb(near_hit), og_mb(near_a), og_mb(near_b)
    SQ[...] = jnp.zeros_like(SQ)

    def grads(near, far, k, q, u, counted):
        for h in (0, 1):
            cols = slice(h * HALF, (h + 1) * HALF)
            if u == 1:
                p = dot_tn(near[k, near_a], OG[h, mb_a])
                p = p + dot_tn(near[k, near_b], OG[h, mb_b])
            else:
                p = dot_tn(near[k, near_hit], OG[h, mb_hit])
                p = p + dot_tn(far[k], OG[h, yf])
            G[q, u, :, cols] = p.astype(jnp.bfloat16)
            if counted:
                SQ[u : u + 1, cols] += jnp.sum(p * p, axis=0, keepdims=True)

    def far_relay(k):
        if k == OWN - 1:
            for frm in (MINUS, PLUS):
                part = pl.ds(pl.multiple_of(c * SLAB + frm * (SLAB // 2), SLAB // 2), SLAB // 2)
                r = FAR.at[k, part]
                remote(r, r, sh.at[frm], rh.at[frm], ydev[frm]).wait_recv()
        else:
            y_far_wait(FAR, k, k)
        relay(FAR.at[k, slab(c)], FAR, k, k, 3).start()

    def start_extra(slot, _):
        src = XNEAR.at[slot, 0, slab(c)]
        g = OWN + slot
        remote(src, src, sx.at[0], rx.at[slot], xdev[0]).wait_recv()
        y_send(src, XNEAR, slot, g, MINUS).start()
        y_send(src, XNEAR, slot, g, PLUS).start()
        relay(src, XNEAR, slot, g, 0).start()
        return 0

    for k in range(OWN):
        grads(NEAR, FAR, k, k, 1, True)
        far_relay(k)
        if k == 2:
            lax.fori_loop(0, extras, start_extra, 0)
    for k in range(OWN):
        relay_wait(FAR, k, k, 3)
        grads(NEAR, FAR, k, k, 0, True)

    far_one = user_far.astype(jnp.float32)
    far_zero = 1.0 - far_one
    sums = jnp.zeros((8, 128), jnp.float32)
    for j in range(8):
        sums = sums + SQ[:, j * 128 : (j + 1) * 128]
    S2[...] = jnp.zeros_like(S2)
    S2[0:1] = sums[0:1] * far_zero + sums[1:2] * far_one
    S2[1:2] = sums[0:1] * far_one + sums[1:2] * far_zero

    def row_copy(d):
        p = lax.rem(row + d, 16)
        return remote(S2, R2.at[row], a2s.at[d], a2r.at[row], (lax.div(p, 4), lax.rem(p, 4), y, c))

    def row_start(d, _):
        row_copy(d).start()
        return 0

    def row_wait(d, _):
        p = lax.rem(row + d, 16)
        remote(S2, R2.at[p], a2s.at[d], a2r.at[p], sdev).wait_recv()
        return 0

    lax.fori_loop(1, 16, row_start, 0)
    R2[row] = S2[...]

    def extra_middle(slot, _):
        g = OWN + slot
        for frm in (MINUS, PLUS):
            y_wait(XNEAR, slot, g, frm)

            @pl.when(slot == frm)
            def _():
                y_forward(XNEAR, XFAR, slot, g, frm).start()

            relay(XNEAR.at[slot, place_of[frm], slab(c)], XNEAR, slot, g, 1 + frm).start()
        return 0

    lax.fori_loop(0, extras, extra_middle, 0)
    lax.fori_loop(1, 16, row_wait, 0)
    total = R2[0]
    for j in range(1, 16):
        total = total + R2[j]
    S1[...] = total

    def col_copy(d):
        p = lax.rem(col + d, 8)
        return remote(S1, R1.at[col], a1s.at[d], a1r.at[col], (z, x, lax.div(p, 2), lax.rem(p, 2)))

    def col_start(d, _):
        col_copy(d).start()
        return 0

    def col_wait(d, _):
        p = lax.rem(col + d, 8)
        remote(S1, R1.at[p], a1s.at[d], a1r.at[p], sdev).wait_recv()
        return 0

    lax.fori_loop(1, 8, col_start, 0)
    R1[col] = S1[...]

    def extra_far(slot, _):
        g = OWN + slot
        y_far_wait(XFAR, slot, g)
        relay(XFAR.at[slot, slab(c)], XFAR, slot, g, 3).start()
        return 0

    def extra_near_wait(slot, _):
        for kind in (0, 1, 2, 3):
            relay_wait(XFAR if kind == 3 else XNEAR, slot, OWN + slot, kind)
        return 0

    lax.fori_loop(0, extras, extra_far, 0)
    lax.fori_loop(0, extras, extra_near_wait, 0)

    def extra_grads(slot, _):
        grads(XNEAR, XFAR, slot, OWN + slot, 1, False)
        grads(XNEAR, XFAR, slot, OWN + slot, 0, False)
        return 0

    lax.fori_loop(0, extras, extra_grads, 0)
    lax.fori_loop(1, 8, col_wait, 0)
    total = R1[0]
    for j in range(1, 8):
        total = total + R1[j]
    factor = TARGET / jnp.sqrt(jnp.sum(total, axis=1, keepdims=True) + 1e-06)
    f_hit = factor[0:1, :] * far_zero + factor[1:2, :] * far_one
    f_other = factor[0:1, :] * far_one + factor[1:2, :] * far_zero

    right = x >= 2
    s1 = jnp.where(inner, 8, jnp.where(right, 0, 4))
    s2 = jnp.where(right, jnp.where(inner, 0, 1), 5)
    shared = [jnp.int32(7), s1, s2, s2 + 1]

    def give_back(direction):
        q = 0 if direction == PLUS else OWN - 1
        return remote(BACK, out.at[pl.ds(q * CH, CH)], ret_s, ret_r, xdev[direction])

    def chunk_of(t, i):
        return jnp.where(t == 0, shared[i], x + i)

    def gram_rows(src, i):
        r = slice(i * CH, (i + 1) * CH)
        t = dot_nt(src[r], src[i * CH :]).astype(jnp.bfloat16)
        A[r, i * CH :] = t
        for j in range(i + 1, 4):
            A[j * CH : (j + 1) * CH, r] = t[:, (j - i) * CH : (j - i + 1) * CH].T

    def finish(rows, gram):
        done = (1.5 * rows.astype(jnp.float32) - 0.5 * dot_nn(gram, X1[...])) * LAST_SCALE
        return done.astype(jnp.bfloat16)

    def put(t, i, value):
        out[pl.ds(pl.multiple_of(chunk_of(t, i) * CH, CH), CH)] = value

    def task(t, _):
        for i in range(4):
            q = chunk_of(t, i)
            X[i * CH : (i + 1) * CH] = (
                f_hit * G[q, 0].astype(jnp.float32) + f_other * G[q, 1].astype(jnp.float32)
            ).astype(jnp.bfloat16)
        for i in range(4):
            gram_rows(X, i)
        for i in range(4):
            r = slice(i * CH, (i + 1) * CH)
            X1[r] = (1.5 * X[r].astype(jnp.float32) - 0.5 * dot_nn(A[r], X[...])).astype(jnp.bfloat16)

        half = jnp.logical_and(t == 0, inner)

        @pl.when(half)
        def _():
            for i in (2, 3):
                r = slice(i * CH, (i + 1) * CH)
                put(t, i, finish(X1[r], dot_nt(X1[r], X1[...]).astype(jnp.bfloat16)))

        @pl.when(jnp.logical_not(half))
        def _():
            gram_rows(X1, 0)
            first = finish(X1[0:CH], A[0:CH])

            @pl.when(t == 0)
            def _():
                BACK[...] = first

                @pl.when(x == 0)
                def _():
                    give_back(PLUS).start()

                @pl.when(x == 3)
                def _():
                    give_back(MINUS).start()

            @pl.when(t == 1)
            def _():
                put(t, 0, first)

            for i in (1, 2, 3):
                gram_rows(X1, i)
            for i in (1, 2, 3):
                r = slice(i * CH, (i + 1) * CH)
                put(t, i, finish(X1[r], A[r]))

        return 0

    lax.fori_loop(0, 2, task, 0)

    @pl.when(x == 0)
    def _():
        give_back(PLUS).wait_send()

    @pl.when(x == 3)
    def _():
        give_back(MINUS).wait_send()

    @pl.when(x == 1)
    def _():
        give_back(PLUS).wait_recv()

    @pl.when(x == 2)
    def _():
        give_back(MINUS).wait_recv()

    @pl.when(inner)
    def _():
        for k in range(3):
            extra(0, 0, MINUS, k).wait_send()

    for h in (0, 1):
        for d in (MINUS, PLUS):
            first_send(h, d).wait_send()
            first_forward(h, d).wait_send()
            for slot in range(4):
                second_send(h, slot, d).wait_send()
                second_forward(h, slot, d).wait_send()

    def drain(k, _):
        for d in (MINUS, PLUS):
            y_send(own_src(k), NEAR, k, k, d).wait_send()
        for kind in range(4):
            relay(own_src(k), FAR if kind == 3 else NEAR, k, k, kind).wait_send()

        @pl.when(k < OWN - 1)
        def _():
            y_forward(NEAR, FAR, k, k, MINUS).wait_send()

        return 0

    lax.fori_loop(0, OWN, drain, 0)
    split_forward(MINUS).wait_send()
    split_forward(PLUS).wait_send()

    def drain_extra(slot, _):
        src = XNEAR.at[slot, 0, slab(c)]
        g = OWN + slot
        for d in (MINUS, PLUS):
            y_send(src, XNEAR, slot, g, d).wait_send()
        for kind in range(4):
            relay(src, XFAR if kind == 3 else XNEAR, slot, g, kind).wait_send()
        y_forward(XNEAR, XFAR, slot, g, MINUS).wait_send()
        return 0

    lax.fori_loop(0, extras, drain_extra, 0)

    def drain_col(d, _):
        col_copy(d).wait_send()
        return 0

    def drain_row(d, _):
        row_copy(d).wait_send()
        return 0

    lax.fori_loop(1, 8, drain_col, 0)
    lax.fori_loop(1, 16, drain_row, 0)


def per_device(inputs, out_grads, user_ids):
    dma = pltpu.SemaphoreType.DMA
    n = OWN + 2
    bf16, f32 = jnp.bfloat16, jnp.float32
    return pl.pallas_call(
        kernel,
        out_shape=jax.ShapeDtypeStruct((OWN * CH, BLOCK), bf16),
        in_specs=[
            pl.BlockSpec(memory_space=pltpu.SMEM),
            pl.BlockSpec(memory_space=pl.ANY),
            pl.BlockSpec(memory_space=pl.ANY),
        ],
        out_specs=pl.BlockSpec(memory_space=pltpu.VMEM),
        scratch_shapes=[
            pltpu.VMEM((OWN, 3, MB, CH), bf16),
            pltpu.VMEM((OWN, MB, CH), bf16),
            pltpu.VMEM((2, 3, MB, CH), bf16),
            pltpu.VMEM((2, MB, CH), bf16),
            pltpu.VMEM((2, 4, MB, HALF), bf16),
            pltpu.VMEM((n, 2, CH, BLOCK), bf16),
            pltpu.VMEM((BLOCK, BLOCK), bf16),
            pltpu.VMEM((BLOCK, BLOCK), bf16),
            pltpu.VMEM((BLOCK, BLOCK), bf16),
            pltpu.VMEM((CH, BLOCK), bf16),
            pltpu.VMEM((8, BLOCK), f32),
            pltpu.VMEM((8, 128), f32),
            pltpu.VMEM((8, 8, 128), f32),
            pltpu.VMEM((8, 128), f32),
            pltpu.VMEM((16, 8, 128), f32),
            dma((2, n)), dma((2, n)), dma((n,)), dma((n,)), dma((2,)), dma((2,)), dma((4, n)), dma((4, n)), dma((n,)), dma((3,)), dma((2,)),
            dma((2, 2)), dma((2, 2)), dma((2, 2)), dma((2, 2)),
            dma((2, 4, 2)), dma((2, 4, 2)), dma((2, 4, 2)), dma((2, 4, 2)), dma((2,)),
            dma((8,)), dma((8,)), dma((16,)), dma((16,)), dma, dma,
        ],
        compiler_params=pltpu.CompilerParams(
            collective_id=0, has_side_effects=True, vmem_limit_bytes=44 * 1024 * 1024
        ),
    )(user_ids, inputs, out_grads)


def solution(mesh):
    torus = Mesh(mesh.devices.reshape(4, 4, 4, 2), ("z", "x", "y", "c"))
    return jax.shard_map(
        per_device,
        mesh=torus,
        in_specs=(P(("y", "c"), ("z", "x")), P(("z", "x"), ("y", "c")), P()),
        out_specs=P(("z", "x"), ("y", "c")),
        check_vma=False,
    )
```

time: 88.4 us -> 72.5 us (0.82)
  Pallas kernels: 84 us -> 67.3 us
    pallas_call x1, Pallas kernels: 84 us -> 67.3 us  [per_device(): pl.pallas_call(kernel, out_shape=jax.ShapeDtypeStruct((OWN * CH, BLOCK),...]
    unnamed x1 -> x7, local copies, waits for them, and re-layouts: 4.25 us -> 4.52 us
where the time goes in v2:
time: 72.5 us; the launch traced here: 71.9 us
  Pallas kernels  67.3 us (93%)
  local copies, waits for them, and re-layouts  4.52 us (6%)
    pallas_call x1, Pallas kernels, per_device(): pl.pallas_call(kernel, out_shape=jax.ShapeDtypeStruct((OWN * CH, BLOCK),...  67.3 us
    unnamed x7, local copies, waits for them, and re-layouts  4.52 us

profile of v2, /device:TPU:1, one launch (start us, length us, event | category | flops | bytes accessed | tf_op | source)
XLA Modules:
  0.0 71.9 jit_solution(14668002220288570572)
XLA Ops:
  0.0 0.0 copy-start
  0.0 1.1 %copy-done = bf16[192,1792]{1,0:T(8,128)(2,1)S(1)} copy-done((bf16[192,1792]{1,0:T(8,128)(2,1)S(1)}, bf16[192,1792]{1,0:T(8,128)(2,1)}, u32[]{:S(2)}) %copy-start) | copy-done | bytes 688152
  1.1 0.0 copy-start.1
  1.1 0.9 %copy-done.1 = bf16[96,1024]{1,0:T(8,128)(2,1)S(1)} copy-done((bf16[96,1024]{1,0:T(8,128)(2,1)S(1)}, bf16[96,1024]{1,0:T(8,128)(2,1)}, u32[]{:S(2)}) %copy-start.1) | copy-done | bytes 196632
  2.0 0.0 copy-start.2
  2.0 0.7 copy-done.2
  2.7 67.3 %shard_map.37 = bf16[1792,1024]{1,0:T(8,128)(2,1)S(1)} custom-call(s32[4]{0:T(128)S(1)} %copy-done.2, bf16[192,1792]{1,0:T(8,128)(2,1)S(1)} %copy-done, bf16[96,1024]{1,0:T(8,128)(2,1)S(1)} %copy-done.1), custom_call_target="tpu_custom_call" | custom-call | tf_op jit(solution)/shard_map/pallas_call | solution.py:570
  70.0 1.8 %copy.5 = bf16[1792,1024]{1,0:T(8,128)(2,1)} copy(bf16[1792,1024]{1,0:T(8,128)(2,1)S(1)} %shard_map.37) | data formatting | bytes 7340032
Async XLA Ops:
  0.0 1.1 %copy-start = (bf16[192,1792]{1,0:T(8,128)(2,1)S(1)}, bf16[192,1792]{1,0:T(8,128)(2,1)}, u32[]{:S(2)}) copy-start(bf16[192,1792]{1,0:T(8,128)(2,1)} %inp.1) | copy-start | bytes 2064388
  1.1 0.9 %copy-start.1 = (bf16[96,1024]{1,0:T(8,128)(2,1)S(1)}, bf16[96,1024]{1,0:T(8,128)(2,1)}, u32[]{:S(2)}) copy-start(bf16[96,1024]{1,0:T(8,128)(2,1)} %og.1) | copy-start | bytes 589828
  2.0 0.7 copy-start.2

commit v3 on v2

v3 whole, which is shorter than its diff:
```python
import math

import jax
import jax.numpy as jnp
from jax import lax
from jax.experimental import pallas as pl
from jax.experimental.pallas import tpu as pltpu
from jax.sharding import Mesh
from jax.sharding import PartitionSpec as P

FF = 28672
D = 8192
BLOCK = 1024
MICRO = 4
TARGET = 0.15 * math.sqrt(FF * D / BLOCK)
LAST_SCALE = math.sqrt(BLOCK)

MESH = pl.DeviceIdType.MESH
CH = 256
OWN = 7
SLAB = 192
MB = 384
GS = 96
HALF = 512
MINUS, PLUS = 0, 1


def dot_tn(a, b):
    return lax.dot_general(a, b, (((0,), (0,)), ((), ())), preferred_element_type=jnp.float32)


def dot_nt(a, b):
    return lax.dot_general(a, b, (((1,), (1,)), ((), ())), preferred_element_type=jnp.float32)


def dot_nn(a, b):
    return lax.dot_general(a, b, (((1,), (0,)), ((), ())), preferred_element_type=jnp.float32)


def kernel(
    users, inp, og, out,
    uids, NEAR, FAR, XNEAR, XFAR, OG, G, X, X1, A, BACK, SQ, S1, R1, S2, R2,
    us, sy, ry, sf, rf, rh, sb0, rb0, sb3, rb3, lc, sx, rx, sxy, rxy, sxf, rxf, sxb, rxb,
    oa1s, oa1r, of1s, of1r, oa2s, oa2r, of2s, of2r, ol,
    a1s, a1r, a2s, a2r, ret_s, ret_r,
):
    z, x, y, c = (lax.axis_index(a) for a in ("z", "x", "y", "c"))
    zm, zp, zf = (lax.rem(z + d, 4) for d in (3, 1, 2))
    xm, xp, xf = (lax.rem(x + d, 4) for d in (3, 1, 2))
    ym, yp, yf = (lax.rem(y + d, 4) for d in (3, 1, 2))
    sib = 1 - c
    inner = jnp.logical_or(x == 1, x == 2)
    extras = jnp.where(inner, 2, 1)
    col = y * 2 + c
    row = z * 4 + x

    barrier = pltpu.get_barrier_semaphore()
    for dev in ((z, x, ym, c), (z, x, yp, c), (z, xm, y, c), (z, xp, y, c), (zm, x, y, c), (zp, x, y, c), (z, x, y, sib)):
        pl.semaphore_signal(barrier, inc=1, device_id=dev, device_id_type=MESH)
    pl.semaphore_wait(barrier, 7)

    def remote(src, dst, ss, rs, dev):
        return pltpu.make_async_remote_copy(
            src_ref=src, dst_ref=dst, send_sem=ss, recv_sem=rs, device_id=dev, device_id_type=MESH
        )

    ydev = [(z, x, ym, c), (z, x, yp, c)]
    xdev = [(z, xm, y, c), (z, xp, y, c)]
    zdev = [(zm, x, y, c), (zp, x, y, c)]
    sdev = (z, x, y, sib)

    def slab(cc):
        return pl.ds(pl.multiple_of(cc * SLAB, SLAB), SLAB)

    def extra(src_chunk, slot, direction, k):
        return remote(
            inp.at[:, pl.ds(src_chunk * CH, CH)], XNEAR.at[slot, 0, slab(c)], sx.at[k], rx.at[slot], xdev[direction]
        )

    def start_shared():
        @pl.when(x == 1)
        def _():
            extra(5, 0, PLUS, 0).start()
            extra(0, 0, MINUS, 1).start()
            extra(6, 1, PLUS, 2).start()

        @pl.when(x == 2)
        def _():
            extra(0, 0, MINUS, 0).start()
            extra(6, 0, PLUS, 1).start()
            extra(1, 1, MINUS, 2).start()

    users_copy = pltpu.make_async_copy(users, uids, us)
    users_copy.start()

    def grow(zz, xx):
        return zz, pl.ds(pl.multiple_of(xx * GS, GS), GS)

    def gpart(zz, xx, part):
        return zz, pl.ds(pl.multiple_of(xx * GS + part * (GS // 2), GS // 2), GS // 2)

    first_dev = [xdev, zdev]
    second_dev = [zdev, xdev]

    def along_first(h, d):
        if h == 0:
            return (z, [x, xm, xp, xf][d])
        return ([z, zm, zp, zf][d], x)

    def second_of(h, slot, d):
        zz, xx = along_first(h, slot)
        if h == 0:
            return ([z, zm, zp, zf][d], xx)
        return (zz, [x, xm, xp, xf][d])

    def first_send(h, direction):
        r = grow(z, x)
        return remote(
            og.at[:, pl.ds(h * HALF, HALF)], OG.at[h, r[0], r[1]], oa1s, oa1r.at[h, 1 - direction],
            first_dev[h][direction],
        )

    def first_wait(h, frm):
        r = grow(*along_first(h, 1 + frm))
        remote(OG.at[h, r[0], r[1]], OG.at[h, r[0], r[1]], oa1s, oa1r.at[h, frm], first_dev[h][frm]).wait_recv()

    def first_forward(h, frm):
        r = gpart(*along_first(h, 1 + frm), frm)
        return remote(
            OG.at[h, r[0], r[1]], OG.at[h, r[0], r[1]], of1s, of1r.at[h], first_dev[h][1 - frm]
        )

    def first_far_wait(h):
        r = grow(*along_first(h, 3))
        r = OG.at[h, r[0], r[1]]
        remote(r, r, of1s, of1r.at[h], first_dev[h][0]).wait_recv()

    def second_send(h, slot, direction):
        r = grow(*along_first(h, slot))
        src = og.at[:, pl.ds(h * HALF, HALF)] if slot == 0 else OG.at[h, r[0], r[1]]
        return remote(
            src, OG.at[h, r[0], r[1]], oa2s, oa2r.at[h, slot, 1 - direction], second_dev[h][direction]
        )

    def second_wait(h, slot, frm):
        r = grow(*second_of(h, slot, 1 + frm))
        remote(
            OG.at[h, r[0], r[1]], OG.at[h, r[0], r[1]], oa2s, oa2r.at[h, slot, frm], second_dev[h][frm]
        ).wait_recv()

    def second_forward(h, slot, frm):
        r = gpart(*second_of(h, slot, 1 + frm), frm)
        return remote(
            OG.at[h, r[0], r[1]], OG.at[h, r[0], r[1]], of2s, of2r, second_dev[h][1 - frm]
        )

    def second_far_wait():
        r = OG.at[0, 0:2]
        remote(r, r, of2s, of2r, xdev[0]).wait_recv()

    for h in (0, 1):
        for d in (MINUS, PLUS):
            first_send(h, d).start()
    for h in (0, 1):
        for d in (MINUS, PLUS):
            second_send(h, 0, d).start()

    place_of = (2, 1)

    def own_src(k):
        return inp.at[:, pl.ds(pl.multiple_of(k * CH, CH), CH)]

    def y_send(src, buf, k, ss, rs, direction):
        return remote(src, buf.at[k, place_of[1 - direction], slab(c)], ss, rs.at[1 - direction, k], ydev[direction])

    def y_wait(buf, k, rs, frm):
        r = buf.at[k, place_of[frm], slab(c)]
        remote(r, r, sf, rs.at[frm, k], ydev[frm]).wait_recv()

    def y_forward(buf, dst, k, ss, rs, frm):
        return remote(buf.at[k, place_of[frm], slab(c)], dst.at[k, slab(c)], ss, rs.at[k], ydev[1 - frm])

    def split_forward(frm):
        k = OWN - 1
        part = pl.ds(pl.multiple_of(c * SLAB + frm * (SLAB // 2), SLAB // 2), SLAB // 2)
        return remote(NEAR.at[k, place_of[frm], part], FAR.at[k, part], sf, rh.at[frm], ydev[1 - frm])

    def y_far_wait(dst, k, rs):
        r = dst.at[k, slab(c)]
        remote(r, r, sf, rs.at[k], ydev[0]).wait_recv()

    def relay(src, dst, k, ss, rs, kind):
        r = slab(c)
        return remote(src, dst.at[k, r] if kind == 3 else dst.at[k, (0, 2, 1)[kind], r], ss, rs, sdev)

    def relay_wait(dst, k, rs, kind):
        r = slab(sib)
        r = dst.at[k, r] if kind == 3 else dst.at[k, (0, 2, 1)[kind], r]
        remote(r, r, sf, rs, sdev).wait_recv()

    def local(k):
        return pltpu.make_async_copy(own_src(k), NEAR.at[k, 0, slab(c)], lc)

    def start_own(k, _):
        y_send(own_src(k), NEAR, k, sy, ry, MINUS).start()
        y_send(own_src(k), NEAR, k, sy, ry, PLUS).start()
        return 0

    lax.fori_loop(0, OWN, start_own, 0)

    def og_local(h):
        return pltpu.make_async_copy(og.at[:, pl.ds(h * HALF, HALF)], OG.at[(h, *grow(z, x))], ol.at[h])

    og_local(0).start()
    og_local(1).start()

    def start_near(k, _):
        local(k).start()
        relay(own_src(k), NEAR, k, sb0, rb0, 0).start()
        return 0

    lax.fori_loop(0, OWN, start_near, 0)

    for h in (1, 0):
        for frm in (MINUS, PLUS):
            first_wait(h, frm)
            first_forward(h, frm).start()
            for d in (MINUS, PLUS):
                second_send(h, 1 + frm, d).start()
    for h in (1, 0):
        for frm in (MINUS, PLUS):
            second_wait(h, 0, frm)
            second_forward(h, 0, frm).start()
    for h in (1, 0):
        first_far_wait(h)
        for d in (MINUS, PLUS):
            second_send(h, 3, d).start()
    for slot in (1, 2, 3):
        for h in (1, 0):
            for frm in (MINUS, PLUS):
                second_wait(h, slot, frm)
                second_forward(h, slot, frm).start()

    start_shared()

    def middle(k, _):
        for frm in (MINUS, PLUS):
            y_wait(NEAR, k, ry, frm)

            @pl.when(jnp.logical_and(lax.rem(k, 2) == frm, k < OWN - 1))
            def _():
                y_forward(NEAR, FAR, k, sf, rf, frm).start()

            relay(NEAR.at[k, place_of[frm], slab(c)], NEAR, k, sb0, rb0, 1 + frm).start()
        return 0

    lax.fori_loop(0, OWN, middle, 0)
    split_forward(MINUS).start()
    split_forward(PLUS).start()

    second_far_wait()
    og_local(0).wait()
    og_local(1).wait()

    own_slabs = NEAR.at[:, 0, slab(c)]
    pltpu.make_async_copy(own_slabs, own_slabs, lc).wait()
    sibling_slabs = NEAR.at[:, :, slab(sib)]
    remote(sibling_slabs, sibling_slabs, sb0, rb0, sdev).wait_recv()

    users_copy.wait()
    user_far = uids[yf]
    d1 = lax.rem(uids[yp] + user_far, 2)
    d2 = lax.rem(uids[ym] + user_far, 2)
    near_hit = (1 - d1) + 2 * d1 * (1 - d2)
    near_a = 1 - jnp.minimum(near_hit, 1)
    near_b = 2 - lax.div(near_hit, 2)

    def og_mb(place):
        return lax.rem(y + place + lax.div(place, 2), 4)

    mb_hit, mb_a, mb_b = og_mb(near_hit), og_mb(near_a), og_mb(near_b)
    SQ[...] = jnp.zeros_like(SQ)

    def grads(near, far, k, q, u, counted):
        for h in (0, 1):
            cols = slice(h * HALF, (h + 1) * HALF)
            if u == 1:
                rows_in = (near[k, near_a], near[k, near_b])
                rows_out = (OG[h, mb_a], OG[h, mb_b])
            else:
                rows_in = (near[k, near_hit], far[k])
                rows_out = (OG[h, mb_hit], OG[h, yf])
            p = dot_tn(jnp.concatenate(rows_in, axis=0), jnp.concatenate(rows_out, axis=0))
            G[q, u, :, cols] = p.astype(jnp.bfloat16)
            if counted:
                squares = p * p
                eight = squares[0:8]
                for e in range(1, CH // 8):
                    eight = eight + squares[8 * e : 8 * e + 8]
                SQ[u, :, cols] += eight

    def far_relay(k):
        if k == OWN - 1:
            for frm in (MINUS, PLUS):
                part = pl.ds(pl.multiple_of(c * SLAB + frm * (SLAB // 2), SLAB // 2), SLAB // 2)
                r = FAR.at[k, part]
                remote(r, r, sf, rh.at[frm], ydev[frm]).wait_recv()
        else:
            y_far_wait(FAR, k, rf)
        relay(FAR.at[k, slab(c)], FAR, k, sb3, rb3.at[k], 3).start()

    def start_extra(slot, _):
        src = XNEAR.at[slot, 0, slab(c)]
        remote(src, src, sx.at[0], rx.at[slot], xdev[0]).wait_recv()
        y_send(src, XNEAR, slot, sxy.at[MINUS, slot], rxy, MINUS).start()
        y_send(src, XNEAR, slot, sxy.at[PLUS, slot], rxy, PLUS).start()
        relay(src, XNEAR, slot, sxb.at[0, slot], rxb.at[0, slot], 0).start()
        return 0

    for k in range(OWN):
        grads(NEAR, FAR, k, k, 1, True)
        far_relay(k)
        if k == 2:
            lax.fori_loop(0, extras, start_extra, 0)
    for k in range(OWN):
        relay_wait(FAR, k, rb3.at[k], 3)
        grads(NEAR, FAR, k, k, 0, True)

    far_one = user_far.astype(jnp.float32)
    far_zero = 1.0 - far_one
    sums = []
    for u in (0, 1):
        lanes = SQ[u, :, 0:128]
        for j in range(1, 8):
            lanes = lanes + SQ[u, :, j * 128 : (j + 1) * 128]
        sums.append(jnp.sum(lanes, axis=0, keepdims=True))
    S2[...] = jnp.zeros_like(S2)
    S2[0:1] = sums[0] * far_zero + sums[1] * far_one
    S2[1:2] = sums[0] * far_one + sums[1] * far_zero

    def row_copy(d):
        p = lax.rem(row + d, 16)
        return remote(S2, R2.at[row], a2s, a2r, (lax.div(p, 4), lax.rem(p, 4), y, c))

    def row_start(d, _):
        row_copy(d).start()
        return 0

    lax.fori_loop(1, 16, row_start, 0)
    R2[row] = S2[...]

    def extra_middle(slot, _):
        for frm in (MINUS, PLUS):
            y_wait(XNEAR, slot, rxy, frm)

            @pl.when(slot == frm)
            def _():
                y_forward(XNEAR, XFAR, slot, sxf.at[slot], rxf, frm).start()

            relay(
                XNEAR.at[slot, place_of[frm], slab(c)], XNEAR, slot, sxb.at[1 + frm, slot], rxb.at[1 + frm, slot], 1 + frm
            ).start()
        return 0

    lax.fori_loop(0, extras, extra_middle, 0)
    others = R2.at[0:15]
    remote(others, others, a2s, a2r, sdev).wait_recv()
    total = R2[0]
    for j in range(1, 16):
        total = total + R2[j]
    S1[...] = total

    def col_copy(d):
        p = lax.rem(col + d, 8)
        return remote(S1, R1.at[col], a1s, a1r, (z, x, lax.div(p, 2), lax.rem(p, 2)))

    def col_start(d, _):
        col_copy(d).start()
        return 0

    lax.fori_loop(1, 8, col_start, 0)
    R1[col] = S1[...]

    def extra_far(slot, _):
        y_far_wait(XFAR, slot, rxf)
        relay(XFAR.at[slot, slab(c)], XFAR, slot, sxb.at[3, slot], rxb.at[3, slot], 3).start()
        return 0

    def extra_near_wait(slot, _):
        for kind in (0, 1, 2, 3):
            relay_wait(XFAR if kind == 3 else XNEAR, slot, rxb.at[kind, slot], kind)
        return 0

    lax.fori_loop(0, extras, extra_far, 0)
    lax.fori_loop(0, extras, extra_near_wait, 0)

    def extra_grads(slot, _):
        grads(XNEAR, XFAR, slot, OWN + slot, 1, False)
        grads(XNEAR, XFAR, slot, OWN + slot, 0, False)
        return 0

    lax.fori_loop(0, extras, extra_grads, 0)
    def sent(ref, sem):
        remote(ref, ref, sem, rb0, sdev).wait_send()

    sent(OG.at[0, 0], oa1s)
    sent(OG.at[0, 0, 0 : 2 * GS], of1s)
    sent(OG.at[0], oa2s)
    sent(OG.at[0, 0:2], of2s)
    sent(NEAR.at[:, 0:2, slab(c)], sy)
    sent(NEAR.at[:, :, slab(c)], sb0)
    sent(FAR.at[:, slab(c)], sf)
    sent(FAR.at[:, slab(c)], sb3)
    sent(R2.at[0:15], a2s)

    @pl.when(inner)
    def _():
        for k in range(3):
            sent(XNEAR.at[0, 0, slab(c)], sx.at[k])

    def drain_extra(slot, _):
        r = XNEAR.at[slot, 0, slab(c)]
        for d in (MINUS, PLUS):
            sent(r, sxy.at[d, slot])
        for kind in range(4):
            sent(r, sxb.at[kind, slot])
        sent(r, sxf.at[slot])
        return 0

    lax.fori_loop(0, extras, drain_extra, 0)
    others = R1.at[0:7]
    remote(others, others, a1s, a1r, sdev).wait_recv()
    total = R1[0]
    for j in range(1, 8):
        total = total + R1[j]
    factor = TARGET / jnp.sqrt(jnp.sum(total, axis=1, keepdims=True) + 1e-06)
    f_hit = factor[0:1, :] * far_zero + factor[1:2, :] * far_one
    f_other = factor[0:1, :] * far_one + factor[1:2, :] * far_zero

    right = x >= 2
    s1 = jnp.where(inner, 8, jnp.where(right, 0, 4))
    s2 = jnp.where(right, jnp.where(inner, 0, 1), 5)
    shared = [jnp.int32(7), s1, s2, s2 + 1]

    def give_back(direction):
        q = 0 if direction == PLUS else OWN - 1
        return remote(BACK, out.at[pl.ds(q * CH, CH)], ret_s, ret_r, xdev[direction])

    def chunk_of(t, i):
        return jnp.where(t == 0, shared[i], x + i)

    def gram_rows(src, i):
        r = slice(i * CH, (i + 1) * CH)
        t = dot_nt(src[r], src[i * CH :]).astype(jnp.bfloat16)
        A[r, i * CH :] = t
        for j in range(i + 1, 4):
            A[j * CH : (j + 1) * CH, r] = t[:, (j - i) * CH : (j - i + 1) * CH].T

    def finish(rows, gram):
        done = (1.5 * rows.astype(jnp.float32) - 0.5 * dot_nn(gram, X1[...])) * LAST_SCALE
        return done.astype(jnp.bfloat16)

    def put(t, i, value):
        out[pl.ds(pl.multiple_of(chunk_of(t, i) * CH, CH), CH)] = value

    def task(t, _):
        for i in range(4):
            q = chunk_of(t, i)
            X[i * CH : (i + 1) * CH] = (
                f_hit * G[q, 0].astype(jnp.float32) + f_other * G[q, 1].astype(jnp.float32)
            ).astype(jnp.bfloat16)
        for i in range(4):
            gram_rows(X, i)
        for i in range(4):
            r = slice(i * CH, (i + 1) * CH)
            X1[r] = (1.5 * X[r].astype(jnp.float32) - 0.5 * dot_nn(A[r], X[...])).astype(jnp.bfloat16)

        half = jnp.logical_and(t == 0, inner)

        @pl.when(half)
        def _():
            for i in (2, 3):
                r = slice(i * CH, (i + 1) * CH)
                put(t, i, finish(X1[r], dot_nt(X1[r], X1[...]).astype(jnp.bfloat16)))

        @pl.when(jnp.logical_not(half))
        def _():
            gram_rows(X1, 0)
            first = finish(X1[0:CH], A[0:CH])

            @pl.when(t == 0)
            def _():
                BACK[...] = first

                @pl.when(x == 0)
                def _():
                    give_back(PLUS).start()

                @pl.when(x == 3)
                def _():
                    give_back(MINUS).start()

            @pl.when(t == 1)
            def _():
                put(t, 0, first)

            for i in (1, 2, 3):
                gram_rows(X1, i)
            for i in (1, 2, 3):
                r = slice(i * CH, (i + 1) * CH)
                put(t, i, finish(X1[r], A[r]))

        return 0

    lax.fori_loop(0, 2, task, 0)
    sent(R1.at[0:7], a1s)

    @pl.when(x == 0)
    def _():
        give_back(PLUS).wait_send()

    @pl.when(x == 3)
    def _():
        give_back(MINUS).wait_send()

    @pl.when(x == 1)
    def _():
        give_back(PLUS).wait_recv()

    @pl.when(x == 2)
    def _():
        give_back(MINUS).wait_recv()


def per_device(inputs, out_grads, user_ids):
    dma = pltpu.SemaphoreType.DMA
    n = OWN + 2
    bf16, f32 = jnp.bfloat16, jnp.float32
    return pl.pallas_call(
        kernel,
        out_shape=jax.ShapeDtypeStruct((OWN * CH, BLOCK), bf16),
        in_specs=[pl.BlockSpec(memory_space=pltpu.HBM)] * 3,
        out_specs=pl.BlockSpec(memory_space=pltpu.VMEM),
        scratch_shapes=[
            pltpu.SMEM((MICRO,), jnp.int32),
            pltpu.VMEM((OWN, 3, MB, CH), bf16),
            pltpu.VMEM((OWN, MB, CH), bf16),
            pltpu.VMEM((2, 3, MB, CH), bf16),
            pltpu.VMEM((2, MB, CH), bf16),
            pltpu.VMEM((2, 4, MB, HALF), bf16),
            pltpu.VMEM((n, 2, CH, BLOCK), bf16),
            pltpu.VMEM((BLOCK, BLOCK), bf16),
            pltpu.VMEM((BLOCK, BLOCK), bf16),
            pltpu.VMEM((BLOCK, BLOCK), bf16),
            pltpu.VMEM((CH, BLOCK), bf16),
            pltpu.VMEM((2, 8, BLOCK), f32),
            pltpu.VMEM((8, 128), f32),
            pltpu.VMEM((8, 8, 128), f32),
            pltpu.VMEM((8, 128), f32),
            pltpu.VMEM((16, 8, 128), f32),
            dma, dma, dma((2, OWN)), dma, dma((OWN - 1,)), dma((2,)), dma, dma, dma, dma((OWN,)), dma,
            dma((3,)), dma((2,)), dma((2, 2)), dma((2, 2)), dma((2,)), dma((2,)), dma((4, 2)), dma((4, 2)),
            dma, dma((2, 2)), dma, dma((2,)), dma, dma((2, 4, 2)), dma, dma, dma((2,)),
            dma, dma, dma, dma, dma, dma,
        ],
        compiler_params=pltpu.CompilerParams(
            collective_id=0, has_side_effects=True, vmem_limit_bytes=44 * 1024 * 1024
        ),
    )(*(pltpu.with_memory_space_constraint(v, pltpu.HBM) for v in (user_ids, inputs, out_grads)))


def solution(mesh):
    torus = Mesh(mesh.devices.reshape(4, 4, 4, 2), ("z", "x", "y", "c"))
    return jax.shard_map(
        per_device,
        mesh=torus,
        in_specs=(P(("y", "c"), ("z", "x")), P(("z", "x"), ("y", "c")), P()),
        out_specs=P(("z", "x"), ("y", "c")),
        check_vma=False,
    )
```

time: 72.5 us -> 65.6 us (0.905)
  Pallas kernels: 67.3 us -> 63.2 us
  local copies, waits for them, and re-layouts: 4.52 us -> 1.84 us
    pallas_call x1, Pallas kernels: 67.3 us -> 63.2 us  [per_device(): pl.pallas_call(kernel, out_shape=jax.ShapeDtypeStruct((OWN * CH, BLOCK),...]
    unnamed x7 -> x1, local copies, waits for them, and re-layouts: 4.52 us -> 1.84 us
where the time goes in v3:
time: 65.6 us; the launch traced here: 65 us
  Pallas kernels  63.2 us (96%)
  local copies, waits for them, and re-layouts  1.84 us (3%)
    pallas_call x1, Pallas kernels, per_device(): pl.pallas_call(kernel, out_shape=jax.ShapeDtypeStruct((OWN * CH, BLOCK),...  63.2 us
    unnamed x1, local copies, waits for them, and re-layouts  1.84 us

profile of v3, /device:TPU:1, one launch (start us, length us, event | category | flops | bytes accessed | tf_op | source)
XLA Modules:
  0.0 65.0 jit_solution(17511632130232028948)
XLA Ops:
  0.0 63.2 %shard_map.37 = bf16[1792,1024]{1,0:T(8,128)(2,1)S(1)} custom-call(s32[4]{0:T(128)} %users.1, bf16[192,1792]{1,0:T(8,128)(2,1)} %inp.1, bf16[96,1024]{1,0:T(8,128)(2,1)} %og.1), custom_call_target="tpu_custom_call" | custom-call | tf_op jit(solution)/shard_map/pallas_call | solution.py:539
  63.2 1.8 %copy.5 = bf16[1792,1024]{1,0:T(8,128)(2,1)} copy(bf16[1792,1024]{1,0:T(8,128)(2,1)S(1)} %shard_map.37) | data formatting | bytes 7340032

commit v4 on v3

--- a/solution.py
+++ b/solution.py
@@ -320,7 +320,7 @@
     for k in range(OWN):
         grads(NEAR, FAR, k, k, 1, True)
         far_relay(k)
-        if k == 2:
+        if k == 4:
             lax.fori_loop(0, extras, start_extra, 0)
     for k in range(OWN):
         relay_wait(FAR, k, rb3.at[k], 3)
@@ -362,7 +362,7 @@
             ).start()
         return 0
 
-    lax.fori_loop(0, extras, extra_middle, 0)
+    lax.fori_loop(0, 1, extra_middle, 0)
     others = R2.at[0:15]
     remote(others, others, a2s, a2r, sdev).wait_recv()
     total = R2[0]
@@ -387,19 +387,25 @@
         return 0
 
     def extra_near_wait(slot, _):
-        for kind in (0, 1, 2, 3):
-            relay_wait(XFAR if kind == 3 else XNEAR, slot, rxb.at[kind, slot], kind)
-        return 0
-
+        for kind in (0, 1, 2):
+            relay_wait(XNEAR, slot, rxb.at[kind, slot], kind)
+        return 0
+
+    lax.fori_loop(1, extras, extra_middle, 0)
+    lax.fori_loop(0, extras, extra_near_wait, 0)
+
+    def extra_other(slot, _):
+        grads(XNEAR, XFAR, slot, OWN + slot, 1, False)
+        return 0
+
+    def extra_hit(slot, _):
+        relay_wait(XFAR, slot, rxb.at[3, slot], 3)
+        grads(XNEAR, XFAR, slot, OWN + slot, 0, False)
+        return 0
+
+    lax.fori_loop(0, extras, extra_other, 0)
     lax.fori_loop(0, extras, extra_far, 0)
-    lax.fori_loop(0, extras, extra_near_wait, 0)
-
-    def extra_grads(slot, _):
-        grads(XNEAR, XFAR, slot, OWN + slot, 1, False)
-        grads(XNEAR, XFAR, slot, OWN + slot, 0, False)
-        return 0
-
-    lax.fori_loop(0, extras, extra_grads, 0)
+    lax.fori_loop(0, extras, extra_hit, 0)
     def sent(ref, sem):
         remote(ref, ref, sem, rb0, sdev).wait_send()
 
@@ -442,9 +448,12 @@
     s2 = jnp.where(right, jnp.where(inner, 0, 1), 5)
     shared = [jnp.int32(7), s1, s2, s2 + 1]
 
-    def give_back(direction):
+    def give_back(direction, part):
         q = 0 if direction == PLUS else OWN - 1
-        return remote(BACK, out.at[pl.ds(q * CH, CH)], ret_s, ret_r, xdev[direction])
+        return remote(
+            BACK.at[pl.ds(part * CH // 2, CH // 2)], out.at[pl.ds(q * CH + part * CH // 2, CH // 2)],
+            ret_s.at[part], ret_r.at[part], xdev[direction],
+        )
 
     def chunk_of(t, i):
         return jnp.where(t == 0, shared[i], x + i)
@@ -486,23 +495,24 @@
         @pl.when(jnp.logical_not(half))
         def _():
             gram_rows(X1, 0)
-            first = finish(X1[0:CH], A[0:CH])
 
             @pl.when(t == 0)
             def _():
-                BACK[...] = first
-
-                @pl.when(x == 0)
-                def _():
-                    give_back(PLUS).start()
-
-                @pl.when(x == 3)
-                def _():
-                    give_back(MINUS).start()
+                for part in (0, 1):
+                    r = slice(part * CH // 2, (part + 1) * CH // 2)
+                    BACK[r] = finish(X1[r], A[r])
+
+                    @pl.when(x == 0)
+                    def _():
+                        give_back(PLUS, part).start()
+
+                    @pl.when(x == 3)
+                    def _():
+                        give_back(MINUS, part).start()
 
             @pl.when(t == 1)
             def _():
-                put(t, 0, first)
+                put(t, 0, finish(X1[0:CH], A[0:CH]))
 
             for i in (1, 2, 3):
                 gram_rows(X1, i)
@@ -517,19 +527,23 @@
 
     @pl.when(x == 0)
     def _():
-        give_back(PLUS).wait_send()
+        for part in (0, 1):
+            give_back(PLUS, part).wait_send()
 
     @pl.when(x == 3)
     def _():
-        give_back(MINUS).wait_send()
+        for part in (0, 1):
+            give_back(MINUS, part).wait_send()
 
     @pl.when(x == 1)
     def _():
-        give_back(PLUS).wait_recv()
+        for part in (0, 1):
+            give_back(PLUS, part).wait_recv()
 
     @pl.when(x == 2)
     def _():
-        give_back(MINUS).wait_recv()
+        for part in (0, 1):
+            give_back(MINUS, part).wait_recv()
 
 
 def per_device(inputs, out_grads, user_ids):
@@ -561,7 +575,7 @@
             dma, dma, dma((2, OWN)), dma, dma((OWN - 1,)), dma((2,)), dma, dma, dma, dma((OWN,)), dma,
             dma((3,)), dma((2,)), dma((2, 2)), dma((2, 2)), dma((2,)), dma((2,)), dma((4, 2)), dma((4, 2)),
             dma, dma((2, 2)), dma, dma((2,)), dma, dma((2, 4, 2)), dma, dma, dma((2,)),
-            dma, dma, dma, dma, dma, dma,
+            dma, dma, dma, dma, dma((2,)), dma((2,)),
         ],
         compiler_params=pltpu.CompilerParams(
             collective_id=0, has_side_effects=True, vmem_limit_bytes=44 * 1024 * 1024

time: 65.6 us -> 65.5 us (level)
  no operation moved by 1% of the time
where the time goes in v4:
time: 65.5 us; the launch traced here: 65.4 us
  Pallas kernels  63.6 us (97%)
  local copies, waits for them, and re-layouts  1.84 us (3%)
    pallas_call x1, Pallas kernels, per_device(): pl.pallas_call(kernel, out_shape=jax.ShapeDtypeStruct((OWN * CH, BLOCK),...  63.6 us
    unnamed x1, local copies, waits for them, and re-layouts  1.84 us

profile of v4, /device:TPU:1, one launch (start us, length us, event | category | flops | bytes accessed | tf_op | source)
XLA Modules:
  0.0 65.4 jit_solution(17704911020191884152)
XLA Ops:
  0.0 63.6 %shard_map.37 = bf16[1792,1024]{1,0:T(8,128)(2,1)S(1)} custom-call(s32[4]{0:T(128)} %users.1, bf16[192,1792]{1,0:T(8,128)(2,1)} %inp.1, bf16[96,1024]{1,0:T(8,128)(2,1)} %og.1), custom_call_target="tpu_custom_call" | custom-call | tf_op jit(solution)/shard_map/pallas_call | solution.py:553
  63.6 1.8 %copy.5 = bf16[1792,1024]{1,0:T(8,128)(2,1)} copy(bf16[1792,1024]{1,0:T(8,128)(2,1)S(1)} %shard_map.37) | data formatting | bytes 7340032
